TPU v7x, 768 devices: a whole 4x8x12 slice. The times are simulated.
768 devices in a mesh: dp: 48 (over z_hi, y, core), expert: 16 (over z_lo, x).
Axes of the slice: x: 4, y: 8, z: 12 (z_hi: 3, z_lo: 4; z = z_hi * 4 + z_lo), core: 2. Of those that a mesh axis runs over, the one named last changes fastest.
Arguments:
- tokens: bfloat16 [98304, 2048], P(('dp', 'expert')), may hold values from -6 to 6
- routes: int32 [98304, 1], P(('dp', 'expert')), may hold values from 0 to 15; in each aligned block of 128 rows (0 to 127, 128 to 255, ...) at most 10 rows name the same one
- route_gates: float32 [98304, 1], P(('dp', 'expert')), may hold values from 0.1 to 1
- w_gate: bfloat16 [16, 2048, 384], P('expert'), may hold values from -0.125 to 0.125
- w_up: bfloat16 [16, 2048, 384], P('expert'), may hold values from -0.125 to 0.125
- w_down: bfloat16 [16, 384, 2048], P('expert'), may hold values from -0.3125 to 0.3125
- cotangent: bfloat16 [98304, 2048], P(('dp', 'expert')), may hold values from -6 to 6
Outputs:
- mixed: bfloat16 [98304, 2048], P(('dp', 'expert'))
- d_tokens: bfloat16 [98304, 2048], P(('dp', 'expert'))
- d_gates: float32 [98304, 1], P(('dp', 'expert'))
- d_w_down: bfloat16 [16, 384, 2048], P('expert', 'dp')
Inputs may be any that keep to these rules, and one draw needn't show every extreme that they name: `routes`: each token names exactly one expert. Among the rows of one device no expert is named more than 10 times, a bound that some block reaches in some devices' rows; every expert is named somewhere.
All inputs are finite; a program needn't handle non-finite values.
Results may differ from a plain program's by a relative error of at most 0.0058.
Values may be sent and summed in bfloat16 or wider, within the bound.
No kernel may reach another device: no remote copies, remote signals or barrier semaphores. Data moves between devices by JAX's collectives and lax.ppermute only.
A program may use at most 32 MiB of HBM per device.

v0:
```python
import math

import jax
import jax.numpy as jnp
from jax import lax
from jax.sharding import PartitionSpec as P


def send_back(values):
    return lax.all_to_all(values, "expert", split_axis=0, concat_axis=0, tiled=True)


def per_device(tokens, routes, route_gates, w_gate, w_up, w_down, cotangent):
    tok_rows, model_width = tokens.shape
    route_count = routes.shape[1]
    expert_count = w_gate.shape[0] * lax.axis_size("expert")
    capacity = 5 * tok_rows * route_count // (4 * expert_count)
    slot_count = expert_count * capacity
    flattened = routes.reshape(-1)
    route_rows = flattened.shape[0]
    one_hot = (flattened[:, None] == jnp.arange(expert_count, dtype=jnp.int32)[None, :]).astype(
        jnp.int32
    )
    earlier = jnp.cumsum(one_hot, axis=0) - one_hot
    slot_of = jnp.sum(earlier * one_hot, axis=1)
    target = flattened * capacity + slot_of
    source_row = (
        jnp.zeros((slot_count,), jnp.int32).at[target].set(jnp.arange(route_rows, dtype=jnp.int32))
    )
    filled = jnp.zeros((slot_count,), jnp.bool_).at[target].set(True)
    outgoing = jnp.where(
        filled[:, None], tokens[source_row // route_count], jnp.zeros((), tokens.dtype)
    )
    outgoing = outgoing.reshape(expert_count, capacity, model_width)
    gate_matrix = w_gate[0]
    up_matrix = w_up[0]
    down_matrix = w_down[0]
    arrived = lax.all_to_all(outgoing, "expert", split_axis=0, concat_axis=0, tiled=True)
    project_pre_gate = jnp.einsum(
        "scd,df->scf", arrived, gate_matrix, preferred_element_type=jnp.float32
    )
    project_pre_up = jnp.einsum(
        "scd,df->scf", arrived, up_matrix, preferred_element_type=jnp.float32
    )
    hidden = (project_pre_gate * jax.nn.sigmoid(project_pre_gate) * project_pre_up).astype(
        jnp.bfloat16
    )
    expert_out = jnp.einsum(
        "scf,fd->scd", hidden, down_matrix, preferred_element_type=jnp.float32
    ).astype(jnp.bfloat16)
    hidden, returned = (hidden, send_back(expert_out))
    results = (returned, project_pre_gate, project_pre_up, hidden)
    returned = results[0]
    hidden = results[-1]
    out_rows = returned.reshape(slot_count, model_width)[target].reshape(
        tok_rows, route_count, model_width
    )
    mixed = jnp.sum(route_gates[:, :, None] * out_rows.astype(jnp.float32), axis=1).astype(
        jnp.bfloat16
    )
    d_gates = jnp.einsum("td,tkd->tk", cotangent, out_rows, preferred_element_type=jnp.float32)
    weighted = (route_gates[:, :, None] * cotangent[:, None, :].astype(jnp.float32)).astype(
        jnp.bfloat16
    )
    weighted = weighted.reshape(route_rows, model_width)
    grad_send = jnp.where(filled[:, None], weighted[source_row], jnp.zeros((), weighted.dtype))
    grad_send = grad_send.reshape(expert_count, capacity, model_width)
    grad_arrived = lax.all_to_all(grad_send, "expert", split_axis=0, concat_axis=0, tiled=True)
    pre_gate = results[1]
    pre_up = results[2]
    grad_scale = 1.0 / math.sqrt(route_count * tok_rows * lax.axis_size("dp"))
    hidden_rows = hidden.reshape(slot_count, hidden.shape[2])
    grad_rows = grad_arrived.reshape(slot_count, model_width)
    grad_hidden = jnp.einsum(
        "scd,fd->scf", grad_arrived, down_matrix, preferred_element_type=jnp.float32
    )
    sigmoid_gate = jax.nn.sigmoid(pre_gate)
    grad_gate = (
        grad_hidden * pre_up * sigmoid_gate * (1.0 + pre_gate * (1.0 - sigmoid_gate))
    ).astype(jnp.bfloat16)
    grad_up = (grad_hidden * pre_gate * sigmoid_gate).astype(jnp.bfloat16)
    grad_input = jnp.einsum(
        "scf,df->scd", grad_gate, gate_matrix, preferred_element_type=jnp.float32
    ) + jnp.einsum("scf,df->scd", grad_up, up_matrix, preferred_element_type=jnp.float32)
    grad_returned = lax.all_to_all(
        grad_input.astype(jnp.bfloat16), "expert", split_axis=0, concat_axis=0, tiled=True
    )
    product = lax.dot_general(
        hidden_rows, grad_rows, (((0,), (0,)), ((), ())), preferred_element_type=jnp.float32
    )
    down_rows = lax.psum_scatter(product * grad_scale, "dp", scatter_dimension=0, tiled=True)
    input_rows = grad_returned.reshape(slot_count, model_width)[target]
    input_rows = input_rows.reshape(tok_rows, route_count, model_width)
    d_tokens = jnp.sum(input_rows.astype(jnp.float32), axis=1).astype(jnp.bfloat16)
    d_w_down = down_rows.astype(jnp.bfloat16)[None]
    return (mixed, d_tokens, d_gates, d_w_down)


def solution(mesh):
    in_specs = (
        P(("dp", "expert"), None),
        P(("dp", "expert"), None),
        P(("dp", "expert"), None),
        P("expert", None, None),
        P("expert", None, None),
        P("expert", None, None),
        P(("dp", "expert"), None),
    )
    out_specs = (
        P(("dp", "expert"), None),
        P(("dp", "expert"), None),
        P(("dp", "expert"), None),
        P("expert", "dp", None),
    )
    return jax.shard_map(
        per_device, mesh=mesh, in_specs=in_specs, out_specs=out_specs, check_vma=False
    )
```

profile of v0, /device:TPU:1, one launch (start us, length us, event | category | flops | bytes accessed | tf_op | source)
XLA Modules:
  0.0 340.9 jit_solution(3405367958637317868)
XLA Ops:
  7.2 0.9 fusion.19
  8.2 0.8 select_reduce_fusion
  9.0 0.7 fusion.22
  9.7 1.0 scatter_custom_fusion.1
  10.7 1.0 scatter_custom_fusion
  11.8 2.8 gather_fusion
  15.0 34.5 %all_to_all.20 = bf16[16,10,2048]{2,1,0:T(8,128)(2,1)S(1)} all-to-all(bf16[16,10,2048]{2,1,0:T(8,128)(2,1)S(1)} %broadcast_select_fusion.1), channel_id=1, replica_groups=mesh['dp'=48,'expert'=16] {'expert'}, dimensions={0} | all-to-all | bytes 1310720 | tf_op jit(solution)/shard_map/all_to_all | solution.py:38
  49.5 0.7 fusion.9
  50.2 0.7 copy-done.3
  50.9 0.7 fusion.5
  51.6 0.7 copy-done.7
  52.6 0.5 convolution_convert_fusion
  53.1 1.4 copy.18
  54.5 5.6 %all-to-all-start.1 = ((bf16[16,10,2048]{2,1,0:T(8,128)(2,1)}), bf16[16,10,2048]{2,1,0:T(8,128)(2,1)S(1)}, u32[]{:S(2)}, u32[]{:S(2)}) async-start(bf16[16,10,2048]{2,1,0:T(8,128)(2,1)} %copy.18), calls=%async_computation.1 | async-start | bytes 2097152 | tf_op jit(solution)/shard_map/all_to_all | solution.py:10
  60.1 22.1 %all-to-all-done.1 = bf16[16,10,2048]{2,1,0:T(8,128)(2,1)S(1)} async-done(((bf16[16,10,2048]{2,1,0:T(8,128)(2,1)}), bf16[16,10,2048]{2,1,0:T(8,128)(2,1)S(1)}, u32[]{:S(2)}, u32[]{:S(2)}) %all-to-all-start.1) | async-done | bytes 655392 | tf_op jit(solution)/shard_map/all_to_all | solution.py:10
  82.2 0.2 reshape.58
  82.5 0.9 gather_fusion.1
  83.4 2.7 fusion.13
  86.1 1.0 gather_fusion.2
  87.5 32.5 %all_to_all.21 = bf16[16,10,2048]{2,1,0:T(8,128)(2,1)S(1)} all-to-all(bf16[16,10,2048]{2,1,0:T(8,128)(2,1)S(1)} %broadcast_select_fusion), channel_id=1, replica_groups=mesh['dp'=48,'expert'=16] {'expert'}, dimensions={0} | all-to-all | bytes 1310720 | tf_op jit(solution)/shard_map/all_to_all | solution.py:68
  120.0 2.4 bitcast_multiply_fusion
  122.5 0.7 fusion.1
  123.2 0.6 copy-done.2
  124.1 0.8 fusion.7
  124.8 0.6 copy-done.4
  125.5 0.7 fusion
  126.2 0.4 copy.20
  126.6 29.1 %all_to_all.22 = bf16[16,10,2048]{2,1,0:T(8,128)(2,1)S(1)} all-to-all(bf16[16,10,2048]{2,1,0:T(8,128)(2,1)S(1)} %copy.20), channel_id=1, replica_groups=mesh['dp'=48,'expert'=16] {'expert'}, dimensions={0} | all-to-all | bytes 1310720 | tf_op jit(solution)/shard_map/all_to_all | solution.py:85
  155.7 0.2 reshape.59
  155.9 1.7 gather_fusion.3
  157.7 174.9 %reduce-scatter.2.cloned.1.call-done = f32[8,2048]{1,0:T(8,128)} async-done(((f32[384,2048]{1,0:T(8,128)}), f32[8,2048]{1,0:T(8,128)}) %reduce-scatter.2.cloned.1.call-update) | async-done | bytes 65552 | tf_op jit(solution)/shard_map/reduce_scatter | solution.py:91
  332.6 1.5 convert_bitcast_fusion
  (30 shorter events, 1.4 us)
Async XLA Ops:
  7.2 45.4 %copy-start = (bf16[1,384,2048]{2,1,0:T(8,128)(2,1)S(1)}, bf16[1,384,2048]{2,1,0:T(8,128)(2,1)}, u32[]{:S(2)}) copy-start(bf16[1,384,2048]{2,1,0:T(8,128)(2,1)} %param.12) | copy-start | bytes 4718596
  15.0 34.5 %copy-start.1 = (bf16[1,2048,384]{2,1,0:T(8,128)(2,1)S(1)}, bf16[1,2048,384]{2,1,0:T(8,128)(2,1)}, u32[]{:S(2)}) copy-start(bf16[1,2048,384]{2,1,0:T(8,128)(2,1)} %param.10) | copy-start | bytes 4718596
  49.5 1.4 copy-start.3
  50.9 1.6 copy-start.5
  51.6 0.7 copy-start.7
  54.5 27.7 %all-to-all-start.1 = ((bf16[16,10,2048]{2,1,0:T(8,128)(2,1)}), bf16[16,10,2048]{2,1,0:T(8,128)(2,1)S(1)}, u32[]{:S(2)}, u32[]{:S(2)}) async-start(bf16[16,10,2048]{2,1,0:T(8,128)(2,1)} %copy.18), calls=%async_computation.1 | async-start | bytes 2097152 | tf_op jit(solution)/shard_map/all_to_all | solution.py:10
  60.0 272.5 %reduce-scatter.2.cloned.1.call-start = ((), (), s32[]{:S(2)}) async-start(), calls=%async_computation.5 | async-start | bytes 3211264 | tf_op jit(solution)/shard_map/reduce_scatter | solution.py:91
  82.4 1.0 copy-start.9
  122.5 1.4 copy-start.2
  122.5 1.5 copy-start.6
  122.5 1.6 copy-start.8
  124.1 1.4 copy-start.4
Sparse Core Ops, SparseCore 0:
  122.6 209.9 reduce-scatter.1
where the time goes:
time: 341 us
  waiting for transfers between devices  197 us (58%)
  blocking collectives  96.2 us (28%)
  between operations  14.3 us (4%)
  local copies, waits for them, and re-layouts  14.2 us (4%)
  other arithmetic  7.13 us (2%)
  matrix products  6.5 us (2%)
  starting transfers between devices  5.59 us (2%)
    reduce_scatter x1, waiting for transfers between devices, per_device(): lax.psum_scatter(product * grad_scale, 'dp', scatter_dimension=0, tiled=T...  175 us
    all_to_all x1, blocking collectives, per_device(): lax.all_to_all(outgoing, 'expert', split_axis=0, concat_axis=0, tiled=True)  34.5 us
    all_to_all x1, blocking collectives, per_device(): lax.all_to_all(grad_send, 'expert', split_axis=0, concat_axis=0, tiled=True)  32.5 us
    all_to_all x1, blocking collectives, per_device(): lax.all_to_all(grad_input.astype(jnp.bfloat16), 'expert', split_axis=0, c...  29.1 us
    all_to_all x1, waiting for transfers between devices, send_back(): lax.all_to_all(values, 'expert', split_axis=0, concat_axis=0, tiled=True)  22.1 us
  transfers between devices with their start and end apart: 2, of which 2 were waited for; matrix products, arithmetic and copies ran while one was open for 1% of the time, Pallas kernels for 0%

commit v1 on v0

v1 whole, which is shorter than its diff:
```python
import functools
import math

import jax
import jax.numpy as jnp
from jax import lax
from jax.experimental import pallas as pl
from jax.experimental.pallas import tpu as pltpu
from jax.sharding import Mesh
from jax.sharding import PartitionSpec as P

BF = jnp.bfloat16
F32 = jnp.float32
EXPERT = ("zlo", "x")
VMEM_BYTES = 40 * 1024 * 1024


def dot(a, b, ca=1, cb=0):
    return lax.dot_general(a, b, (((ca,), (cb,)), ((), ())), preferred_element_type=F32)


def picks(base, rows, cap, part):
    q = lax.broadcasted_iota(jnp.int32, (rows, base.shape[1]), 0)
    return jnp.where(q == base + part * cap, 1.0, 0.0).astype(BF)


def column(row):
    n = row.shape[1]
    eye = lax.broadcasted_iota(jnp.int32, (n, n), 0) == lax.broadcasted_iota(jnp.int32, (n, n), 1)
    return jnp.sum(jnp.where(eye, row, jnp.zeros((), row.dtype)), axis=1, keepdims=True)


def dispatch_kernel(experts, cap, routes_ref, gates_ref, tok_ref, cot_ref, send_ref, base_ref):
    rows, width = tok_ref.shape
    half = width // 2
    routes = routes_ref[...]
    named = lax.broadcasted_iota(jnp.int32, (experts, rows), 0) == routes
    before = lax.broadcasted_iota(jnp.int32, (rows, rows), 0) < lax.broadcasted_iota(
        jnp.int32, (rows, rows), 1
    )
    earlier = dot(
        jnp.where(named, 1.0, 0.0).astype(BF), jnp.where(before, 1.0, 0.0).astype(BF)
    )
    slot = jnp.sum(jnp.where(named, earlier, 0.0), axis=0, keepdims=True).astype(jnp.int32)
    base = routes * (4 * cap) + slot
    base_ref[...] = jnp.broadcast_to(base, base_ref.shape)
    graded = (column(gates_ref[...]) * cot_ref[...].astype(F32)).astype(BF)
    tok = tok_ref[...]
    sources = jnp.concatenate(
        [tok[:, :half], tok[:, half:], graded[:, :half], graded[:, half:]], axis=0
    )
    slots = send_ref.shape[0]
    pick = jnp.concatenate([picks(base, slots, cap, part) for part in range(4)], axis=1)
    send_ref[...] = dot(pick, sources).astype(BF)


def expert_kernel(
    ranks, cap, scale, place_ref, got_ref, wg_ref, wu_ref, wd_ref, back_ref, keep_ref, give_ref, prod_ref
):
    slots, half = got_ref.shape
    n = ranks * cap
    r = lax.broadcasted_iota(jnp.int32, (n, slots), 0)
    q = lax.broadcasted_iota(jnp.int32, (n, slots), 1)
    got = got_ref[...]
    source = (r // cap) * (4 * cap) + r % cap
    pick = [jnp.where(q == source + part * cap, 1.0, 0.0).astype(BF) for part in range(4)]
    x0, x1, g0, g1 = (dot(p, got).astype(BF) for p in pick)
    x = jnp.concatenate([x0, x1], axis=1)
    g = jnp.concatenate([g0, g1], axis=1)
    pre_gate = dot(x, wg_ref[...])
    pre_up = dot(x, wu_ref[...])
    s = jax.nn.sigmoid(pre_gate)
    hidden = (pre_gate * s * pre_up).astype(BF)
    prod_ref[...] = dot(hidden, g, 0, 0) * scale
    zhi, y, core = place_ref[0], place_ref[1], place_ref[2]
    ring, line, depth, _ = keep_ref.shape
    for k in range(ring):
        for j in range(line):
            chip = lax.rem(zhi + j, line) * ring + lax.rem(y + k, ring)
            mine = pl.multiple_of((2 * chip + core) * depth, depth)
            theirs = pl.multiple_of((2 * chip + 1 - core) * depth, depth)
            keep_ref[k, j] = prod_ref[pl.ds(mine, depth), :]
            give_ref[k, j] = prod_ref[pl.ds(theirs, depth), :].astype(BF)
    out = dot(hidden, wd_ref[...]).astype(BF)
    grad_hidden = dot(g, wd_ref[...], 1, 1)
    grad_gate = (grad_hidden * pre_up * s * (1.0 + pre_gate * (1.0 - s))).astype(BF)
    grad_up = (grad_hidden * pre_gate * s).astype(BF)
    grad_in = (dot(grad_gate, wg_ref[...], 1, 1) + dot(grad_up, wu_ref[...], 1, 1)).astype(BF)
    packed = dot(pick[0], out[:, :half], 0, 0)
    packed += dot(pick[1], out[:, half:], 0, 0)
    packed += dot(pick[2], grad_in[:, :half], 0, 0)
    packed += dot(pick[3], grad_in[:, half:], 0, 0)
    back_ref[...] = packed.astype(BF)


def collect_kernel(cap, base_ref, gates_ref, cot_ref, back_ref, mixed_ref, dtok_ref, dgate_ref):
    rows, width = cot_ref.shape
    half = width // 2
    slots = back_ref.shape[0]
    base = base_ref[0:1, :]
    back = back_ref[...]
    take = [dot(picks(base, slots, cap, part), back, 0, 0) for part in range(4)]
    gate = column(gates_ref[...])
    mixed_ref[:, :half] = (gate * take[0]).astype(BF)
    mixed_ref[:, half:] = (gate * take[1]).astype(BF)
    dtok_ref[:, :half] = take[2].astype(BF)
    dtok_ref[:, half:] = take[3].astype(BF)
    inner = jnp.sum(cot_ref[:, :half].astype(F32) * take[0], axis=1, keepdims=True)
    inner += jnp.sum(cot_ref[:, half:].astype(F32) * take[1], axis=1, keepdims=True)
    eye = lax.broadcasted_iota(jnp.int32, (rows, rows), 0) == lax.broadcasted_iota(
        jnp.int32, (rows, rows), 1
    )
    dgate_ref[...] = jnp.sum(jnp.where(eye, inner, 0.0), axis=0, keepdims=True)


def onchip(x):
    return pltpu.with_memory_space_constraint(x, pltpu.VMEM)


def tree(parts):
    terms = [part.astype(F32) for part in parts]
    while len(terms) > 1:
        terms = [sum(terms[i : i + 2][1:], terms[i]) for i in range(0, len(terms), 2)]
    return terms[0].astype(BF)


def pair_kernel(keep_ref, other_ref, *pair_refs):
    for k, ref in enumerate(pair_refs):
        ref[...] = (keep_ref[k] + other_ref[k].astype(F32)).astype(BF)


def ring_kernel(*refs):
    line = refs[0].shape[0]
    for j in range(line):
        refs[len(refs) - line + j][...] = tree([ref[j] for ref in refs[: len(refs) - line]])


def whole(count):
    return [pl.BlockSpec(memory_space=pltpu.VMEM)] * count


def per_device(tokens, routes, route_gates, w_gate, w_up, w_down, cotangent):
    rows, width = tokens.shape
    ranks = lax.axis_size(EXPERT)
    experts = w_gate.shape[0] * ranks
    ff = w_gate.shape[2]
    dp = lax.axis_size(("zhi", "y", "core"))
    zhi, ring, cores = (lax.axis_size(a) for a in ("zhi", "y", "core"))
    cap = 5 * rows * routes.shape[1] // (4 * experts)
    half = width // 2
    slots = 4 * cap * experts
    route_row = routes.reshape(1, rows)
    gate_row = route_gates.reshape(1, rows)
    send, base = pl.pallas_call(
        functools.partial(dispatch_kernel, experts, cap),
        out_shape=(
            jax.ShapeDtypeStruct((slots, half), BF),
            jax.ShapeDtypeStruct((8, rows), jnp.int32),
        ),
        in_specs=whole(4),
        out_specs=tuple(whole(2)),
        compiler_params=pltpu.CompilerParams(vmem_limit_bytes=VMEM_BYTES),
        name="dispatch",
    )(route_row, gate_row, tokens, cotangent)
    got = lax.all_to_all(
        send.reshape(experts, 4 * cap, half), EXPERT, split_axis=0, concat_axis=0, tiled=True
    )
    depth = ff // dp
    scale = 1.0 / math.sqrt(routes.shape[1] * rows * dp)
    place = jnp.stack([lax.axis_index(a) for a in ("zhi", "y", "core")]).astype(jnp.int32)
    back, keep, give = pl.pallas_call(
        functools.partial(expert_kernel, ranks, cap, scale),
        out_shape=(
            jax.ShapeDtypeStruct((slots, half), BF),
            jax.ShapeDtypeStruct((ring, zhi, depth, width), F32),
            jax.ShapeDtypeStruct((ring, zhi, depth, width), BF),
        ),
        in_specs=[pl.BlockSpec(memory_space=pltpu.SMEM)] + whole(4),
        out_specs=tuple(whole(3)),
        scratch_shapes=[pltpu.VMEM((ff, width), F32)],
        compiler_params=pltpu.CompilerParams(vmem_limit_bytes=VMEM_BYTES),
        name="expert",
    )(place, onchip(got.reshape(slots, half)), w_gate[0], w_up[0], w_down[0])
    returned = lax.all_to_all(
        back.reshape(experts, 4 * cap, half), EXPERT, split_axis=0, concat_axis=0, tiled=True
    )
    other = lax.ppermute(give, "core", [(i, cores - 1 - i) for i in range(cores)])
    tile = jax.ShapeDtypeStruct((zhi, depth, width), BF)
    pairs = pl.pallas_call(
        pair_kernel,
        out_shape=(tile,) * ring,
        in_specs=whole(2),
        out_specs=tuple(whole(ring)),
        compiler_params=pltpu.CompilerParams(vmem_limit_bytes=VMEM_BYTES),
        name="pair",
    )(keep, onchip(other))
    came = [
        lax.ppermute(pairs[k], "y", [(i, (i + k) % ring) for i in range(ring)])
        for k in range(1, ring)
    ]
    tile = jax.ShapeDtypeStruct((depth, width), BF)
    lines = pl.pallas_call(
        ring_kernel,
        out_shape=(tile,) * zhi,
        in_specs=whole(ring),
        out_specs=tuple(whole(zhi)),
        compiler_params=pltpu.CompilerParams(vmem_limit_bytes=VMEM_BYTES),
        name="ringsum",
    )(pairs[0], *came)
    last = [
        lax.ppermute(lines[j], "zhi", [(i, (i + j) % zhi) for i in range(zhi)])
        for j in range(1, zhi)
    ]
    d_w_down = tree([lines[0], *last])[None]
    mixed, d_tokens, d_gates = pl.pallas_call(
        functools.partial(collect_kernel, cap),
        out_shape=(
            jax.ShapeDtypeStruct((rows, width), BF),
            jax.ShapeDtypeStruct((rows, width), BF),
            jax.ShapeDtypeStruct((1, rows), F32),
        ),
        in_specs=whole(4),
        out_specs=tuple(whole(3)),
        compiler_params=pltpu.CompilerParams(vmem_limit_bytes=VMEM_BYTES),
        name="collect",
    )(base, gate_row, cotangent, onchip(returned.reshape(slots, half)))
    return (mixed, d_tokens, d_gates.reshape(rows, 1), d_w_down)


def physical(mesh):
    dp, expert = (mesh.shape[a] for a in ("dp", "expert"))
    sizes = (3, dp // 6, 2, 4, expert // 4)
    return Mesh(mesh.devices.reshape(sizes), ("zhi", "y", "core", "zlo", "x"))


def solution(mesh):
    dp = ("zhi", "y", "core")
    every = P(dp + EXPERT, None)
    weight = P(EXPERT, None, None)
    return jax.shard_map(
        per_device,
        mesh=physical(mesh),
        in_specs=(every, every, every, weight, weight, weight, every),
        out_specs=(every, every, every, P(EXPERT, dp, None)),
        check_vma=False,
    )
```

time: 341 us -> 131 us (0.38)
  waiting for transfers between devices: 197 us -> 41 us
  blocking collectives: 96.2 us -> 0 us
  starting transfers between devices: 5.59 us -> 65.4 us
  between operations: 14.3 us -> 0.83 us
  Pallas kernels: 0 us -> 10.9 us
  matrix products: 6.5 us -> 0 us
  other arithmetic: 7.13 us -> 0.71 us
  local copies, waits for them, and re-layouts: 14.2 us -> 9.56 us
    reduce_scatter x1 -> x0, waiting for transfers between devices: 175 us -> none  [per_device(): lax.psum_scatter(product * grad_scale, 'dp', scatter_dimension=0, tiled=T...]
    all_to_all x3 -> x0, blocking collectives: 96.2 us -> none  [the longest x1 34.5 us: per_device(): lax.all_to_all(outgoing, 'expert', split_axis=0, concat_axis=0, tiled=True)]
    ppermute x0 -> x10, starting transfers between devices: none -> 46.4 us  [the longest x7 28.4 us: per_device(): lax.ppermute(pairs[k], 'y', [(i, (i + k) % ring) for i in range(ring)])]
    ppermute x0 -> x10, waiting for transfers between devices: none -> 14.8 us  [the longest x7 7.24 us: per_device(): lax.ppermute(pairs[k], 'y', [(i, (i + k) % ring) for i in range(ring)])]
    all_to_all x1 -> x2, starting transfers between devices: 5.55 us -> 19.1 us  [the longest x1 10.4 us: per_device(): lax.all_to_all(send.reshape(experts, 4 * cap, half), EXPERT, split_axis=0...]
    pallas_call x0 -> x5, Pallas kernels: none -> 10.9 us  [the longest x1 6.64 us: per_device(): pl.pallas_call(functools.partial(expert_kernel, ranks, cap, scale), out_s...]
    gather x6 -> x0, local copies, waits for them, and re-layouts: 6.91 us -> none  [the longest x2 3 us: per_device(): tokens[source_row // route_count]]
    unnamed x20 -> x22, local copies, waits for them, and re-layouts: 2.95 us -> 9.56 us
  transfers between devices with their start and end apart: 2 -> 12, of which waited for: 2 -> 5; matrix products, arithmetic and copies ran while one was open for 1% -> 1% of each run, Pallas kernels for 0% -> 0%
where the time goes in v1:
time: 131 us; the launch traced here: 128 us
  starting transfers between devices  65.4 us (50%)
  waiting for transfers between devices  41 us (31%)
  Pallas kernels  10.9 us (8%)
  local copies, waits for them, and re-layouts  9.56 us (7%)
    ppermute x7, starting transfers between devices, per_device(): lax.ppermute(pairs[k], 'y', [(i, (i + k) % ring) for i in range(ring)])  28.4 us
    all_to_all x1, waiting for transfers between devices, per_device(): lax.all_to_all(send.reshape(experts, 4 * cap, half), EXPERT, split_axis=0...  26.1 us
    ppermute x2, starting transfers between devices, per_device(): lax.ppermute(lines[j], 'zhi', [(i, (i + j) % zhi) for i in range(zhi)])  13.5 us
    all_to_all x1, starting transfers between devices, per_device(): lax.all_to_all(send.reshape(experts, 4 * cap, half), EXPERT, split_axis=0...  10.4 us
    unnamed x22, local copies, waits for them, and re-layouts  9.56 us
    all_to_all x1, starting transfers between devices, per_device(): lax.all_to_all(back.reshape(experts, 4 * cap, half), EXPERT, split_axis=0...  8.69 us
    ppermute x7, waiting for transfers between devices, per_device(): lax.ppermute(pairs[k], 'y', [(i, (i + k) % ring) for i in range(ring)])  7.24 us
    pallas_call x1, Pallas kernels, per_device(): pl.pallas_call(functools.partial(expert_kernel, ranks, cap, scale), out_s...  6.64 us
  transfers between devices with their start and end apart: 12, of which 5 were waited for; matrix products, arithmetic and copies ran while one was open for 1% of the time, Pallas kernels for 0%

profile of v1, /device:TPU:1, one launch (start us, length us, event | category | flops | bytes accessed | tf_op | source)
XLA Modules:
  0.0 128.3 jit_solution(7112457625216981613)
XLA Ops:
  0.6 1.0 copy-done
  1.7 1.0 copy-done.6
  2.7 0.7 copy-done.7
  3.4 0.7 copy-done.9
  4.0 2.1 %dispatch.1 = (bf16[640,1024]{1,0:T(8,128)(2,1)}, s32[8,128]{1,0:T(8,128)S(1)}) custom-call(s32[1,128]{1,0:T(1,128)S(1)} %bitcast.23, f32[1,128]{1,0:T(1,128)S(1)} %bitcast.21, bf16[128,2048]{1,0:T(8,128)(2,1)S(1)} %copy-done.6, bf16[128,2048]{1,0:T(8,128)(2,1)S(1)} %copy-done), custom_call_target="tpu_custom_call" | custom-call | tf_op jit(solution)/shard_map/dispatch/pallas_call | solution.py:154
  6.2 10.4 %all-to-all-start = ((bf16[16,40,1024]{2,1,0:T(8,128)(2,1)}), bf16[16,40,1024]{2,1,0:T(8,128)(2,1)S(1)}, u32[]{:S(2)}, u32[]{:S(2)}) async-start(bf16[16,40,1024]{2,1,0:T(8,128)(2,1)} %bitcast.5), calls=%async_computation | async-start | bytes 2621440 | tf_op jit(solution)/shard_map/all_to_all | solution.py:165
  16.6 26.1 %all-to-all-done = bf16[16,40,1024]{2,1,0:T(8,128)(2,1)S(1)} async-done(((bf16[16,40,1024]{2,1,0:T(8,128)(2,1)}), bf16[16,40,1024]{2,1,0:T(8,128)(2,1)S(1)}, u32[]{:S(2)}, u32[]{:S(2)}) %all-to-all-start) | async-done | bytes 1310752 | tf_op jit(solution)/shard_map/all_to_all | solution.py:165
  42.8 1.4 %copy-done.2 = bf16[1,2048,384]{2,1,0:T(8,128)(2,1)S(1)} copy-done((bf16[1,2048,384]{2,1,0:T(8,128)(2,1)S(1)}, bf16[1,2048,384]{2,1,0:T(8,128)(2,1)}, u32[]{:S(2)}) %copy-start.2) | copy-done | bytes 1572888
  44.2 1.4 %copy-done.3 = bf16[1,2048,384]{2,1,0:T(8,128)(2,1)S(1)} copy-done((bf16[1,2048,384]{2,1,0:T(8,128)(2,1)S(1)}, bf16[1,2048,384]{2,1,0:T(8,128)(2,1)}, u32[]{:S(2)}) %copy-start.3) | copy-done | bytes 1572888
  45.6 1.4 %copy-done.4 = bf16[1,384,2048]{2,1,0:T(8,128)(2,1)S(1)} copy-done((bf16[1,384,2048]{2,1,0:T(8,128)(2,1)S(1)}, bf16[1,384,2048]{2,1,0:T(8,128)(2,1)}, u32[]{:S(2)}) %copy-start.4) | copy-done | bytes 1572888
  47.0 6.6 %expert.1 = (bf16[640,1024]{1,0:T(8,128)(2,1)S(1)}, f32[8,3,8,2048]{3,2,1,0:T(8,128)S(1)}, bf16[8,3,8,2048]{3,2,1,0:T(8,128)(2,1)S(1)}) custom-call(s32[3]{0:T(128)S(1)} %pad_add_fusion.place_ref, bf16[640,1024]{1,0:T(8,128)(2,1)S(1)} %bitcast.16, bf16[2048,384]{1,0:T(8,128)(2,1)S(1)} %bitcast.17, bf16[2048,384]{1,0:T(8,128)(2,1)S(1)} %bitcast.18, ...), custom_call_target="tpu_custom_call" | custom-call | tf_op jit(solution)/shard_map/expert/pallas_call | solution.py:171
  53.6 1.1 copy-done.5
  54.7 0.9 copy-done.10
  55.6 8.7 %all-to-all-start.1 = ((bf16[16,40,1024]{2,1,0:T(8,128)(2,1)}), bf16[16,40,1024]{2,1,0:T(8,128)(2,1)S(1)}, u32[]{:S(2)}, u32[]{:S(2)}) async-start(bf16[16,40,1024]{2,1,0:T(8,128)(2,1)} %bitcast.20), calls=%async_computation.1 | async-start | bytes 2621440 | tf_op jit(solution)/shard_map/all_to_all | solution.py:184
  64.3 4.4 %collective-permute-start = (bf16[8,3,8,2048]{3,2,1,0:T(8,128)(2,1)}, bf16[8,3,8,2048]{3,2,1,0:T(8,128)(2,1)S(1)}, u32[]{:S(2)}, u32[]{:S(2)}) collective-permute-start(bf16[8,3,8,2048]{3,2,1,0:T(8,128)(2,1)} %copy-done.10), channel_id=1, source_target_pairs={{0,16},{16,0},{1,17},{17,1},{2,18},{18,2},{3,19},{19,3},{4,20},{20... | collective-permute-start | bytes 2359304 | tf_op jit(solution)/shard_map/ppermute | solution.py:187
  68.7 2.1 %collective-permute-done.other_ref = bf16[8,3,8,2048]{3,2,1,0:T(8,128)(2,1)S(1)} collective-permute-done((bf16[8,3,8,2048]{3,2,1,0:T(8,128)(2,1)}, bf16[8,3,8,2048]{3,2,1,0:T(8,128)(2,1)S(1)}, u32[]{:S(2)}, u32[]{:S(2)}) %collective-permute-start) | collective-permute-done | bytes 786464 | tf_op jit(solution)/shard_map/ppermute | solution.py:187
  70.8 0.2 pair.1
  71.0 3.2 %collective-permute-start.1 = (bf16[3,8,2048]{2,1,0:T(8,128)(2,1)S(1)}, bf16[3,8,2048]{2,1,0:T(8,128)(2,1)S(1)}, u32[]{:S(2)}, u32[]{:S(2)}) collective-permute-start(bf16[3,8,2048]{2,1,0:T(8,128)(2,1)S(1)} %get-tuple-element.32), channel_id=1, source_target_pairs={{0,32},{32,64},{64,96},{96,128},{128,160},{160,192},{192,224},{224... | collective-permute-start | bytes 294920 | tf_op jit(solution)/shard_map/ppermute | solution.py:198
  74.2 4.2 %collective-permute-start.2 = (bf16[3,8,2048]{2,1,0:T(8,128)(2,1)S(1)}, bf16[3,8,2048]{2,1,0:T(8,128)(2,1)S(1)}, u32[]{:S(2)}, u32[]{:S(2)}) collective-permute-start(bf16[3,8,2048]{2,1,0:T(8,128)(2,1)S(1)} %get-tuple-element.33), channel_id=1, source_target_pairs={{0,64},{32,96},{64,128},{96,160},{128,192},{160,224},{192,0},{224,... | collective-permute-start | bytes 294920 | tf_op jit(solution)/shard_map/ppermute | solution.py:198
  78.4 4.6 %collective-permute-start.3 = (bf16[3,8,2048]{2,1,0:T(8,128)(2,1)S(1)}, bf16[3,8,2048]{2,1,0:T(8,128)(2,1)S(1)}, u32[]{:S(2)}, u32[]{:S(2)}) collective-permute-start(bf16[3,8,2048]{2,1,0:T(8,128)(2,1)S(1)} %get-tuple-element.34), channel_id=1, source_target_pairs={{0,96},{32,128},{64,160},{96,192},{128,224},{160,0},{192,32},{224,... | collective-permute-start | bytes 294920 | tf_op jit(solution)/shard_map/ppermute | solution.py:198
  83.1 3.5 %collective-permute-start.4 = (bf16[3,8,2048]{2,1,0:T(8,128)(2,1)S(1)}, bf16[3,8,2048]{2,1,0:T(8,128)(2,1)S(1)}, u32[]{:S(2)}, u32[]{:S(2)}) collective-permute-start(bf16[3,8,2048]{2,1,0:T(8,128)(2,1)S(1)} %get-tuple-element.35), channel_id=1, source_target_pairs={{0,128},{32,160},{64,192},{96,224},{128,0},{160,32},{192,64},{224,... | collective-permute-start | bytes 294920 | tf_op jit(solution)/shard_map/ppermute | solution.py:198
  86.6 4.9 %collective-permute-start.5 = (bf16[3,8,2048]{2,1,0:T(8,128)(2,1)S(1)}, bf16[3,8,2048]{2,1,0:T(8,128)(2,1)S(1)}, u32[]{:S(2)}, u32[]{:S(2)}) collective-permute-start(bf16[3,8,2048]{2,1,0:T(8,128)(2,1)S(1)} %get-tuple-element.36), channel_id=1, source_target_pairs={{0,160},{32,192},{64,224},{96,0},{128,32},{160,64},{192,96},{224,1... | collective-permute-start | bytes 294920 | tf_op jit(solution)/shard_map/ppermute | solution.py:198
  91.5 5.0 %collective-permute-start.6 = (bf16[3,8,2048]{2,1,0:T(8,128)(2,1)S(1)}, bf16[3,8,2048]{2,1,0:T(8,128)(2,1)S(1)}, u32[]{:S(2)}, u32[]{:S(2)}) collective-permute-start(bf16[3,8,2048]{2,1,0:T(8,128)(2,1)S(1)} %get-tuple-element.37), channel_id=1, source_target_pairs={{0,192},{32,224},{64,0},{96,32},{128,64},{160,96},{192,128},{224,1... | collective-permute-start | bytes 294920 | tf_op jit(solution)/shard_map/ppermute | solution.py:198
  96.5 3.0 %collective-permute-start.7 = (bf16[3,8,2048]{2,1,0:T(8,128)(2,1)S(1)}, bf16[3,8,2048]{2,1,0:T(8,128)(2,1)S(1)}, u32[]{:S(2)}, u32[]{:S(2)}) collective-permute-start(bf16[3,8,2048]{2,1,0:T(8,128)(2,1)S(1)} %get-tuple-element.38), channel_id=1, source_target_pairs={{0,224},{32,0},{64,32},{96,64},{128,96},{160,128},{192,160},{224,1... | collective-permute-start | bytes 294920 | tf_op jit(solution)/shard_map/ppermute | solution.py:198
  99.5 6.2 %collective-permute-done.6.refs_6_ = bf16[3,8,2048]{2,1,0:T(8,128)(2,1)S(1)} collective-permute-done((bf16[3,8,2048]{2,1,0:T(8,128)(2,1)S(1)}, bf16[3,8,2048]{2,1,0:T(8,128)(2,1)S(1)}, u32[]{:S(2)}, u32[]{:S(2)}) %collective-permute-start.6) | collective-permute-done | bytes 98336 | tf_op jit(solution)/shard_map/ppermute | solution.py:198
  105.7 1.0 collective-permute-done.7.refs_7_
  106.8 0.1 ringsum.1
  106.9 10.3 %collective-permute-start.8 = (bf16[8,2048]{1,0:T(8,128)(2,1)S(1)}, bf16[8,2048]{1,0:T(8,128)(2,1)S(1)}, u32[]{:S(2)}, u32[]{:S(2)}) collective-permute-start(bf16[8,2048]{1,0:T(8,128)(2,1)S(1)} %get-tuple-element.40), channel_id=1, source_target_pairs={{0,256},{256,512},{512,0},{1,257},{257,513},{513,1},{2,258},{258,5... | collective-permute-start | bytes 98312 | tf_op jit(solution)/shard_map/ppermute | solution.py:211
  117.2 3.2 %collective-permute-start.9 = (bf16[8,2048]{1,0:T(8,128)(2,1)S(1)}, bf16[8,2048]{1,0:T(8,128)(2,1)S(1)}, u32[]{:S(2)}, u32[]{:S(2)}) collective-permute-start(bf16[8,2048]{1,0:T(8,128)(2,1)S(1)} %get-tuple-element.41), channel_id=1, source_target_pairs={{0,512},{256,0},{512,256},{1,513},{257,1},{513,257},{2,514},{258,2... | collective-permute-start | bytes 98312 | tf_op jit(solution)/shard_map/ppermute | solution.py:211
  120.4 5.5 %collective-permute-done.9 = bf16[8,2048]{1,0:T(8,128)(2,1)S(1)} collective-permute-done((bf16[8,2048]{1,0:T(8,128)(2,1)S(1)}, bf16[8,2048]{1,0:T(8,128)(2,1)S(1)}, u32[]{:S(2)}, u32[]{:S(2)}) %collective-permute-start.9) | collective-permute-done | bytes 32800 | tf_op jit(solution)/shard_map/ppermute | solution.py:211
  125.9 0.6 fusion
  126.5 1.8 %collect.1 = (bf16[128,2048]{1,0:T(8,128)(2,1)}, bf16[128,2048]{1,0:T(8,128)(2,1)}, f32[1,128]{1,0:T(1,128)}) custom-call(s32[8,128]{1,0:T(8,128)S(1)} %get-tuple-element.23.base_ref, f32[1,128]{1,0:T(1,128)S(1)} %bitcast.22, bf16[128,2048]{1,0:T(8,128)(2,1)S(1)} %copy-done.1, bf16[640,1024]{1,0:T(8,128)(2,1)S(1)} %bitcast.15), custom_call_target="tpu_custom_call" | custom-call | tf_op jit(solution)/shard_map/collect/pallas_call | solution.py:215
  (21 shorter events, 0.1 us)
Async XLA Ops:
  0.6 1.0 copy-start
  1.7 1.0 copy-start.6
  2.7 0.7 copy-start.7
  3.4 0.7 copy-start.9
  6.2 36.6 %all-to-all-start = ((bf16[16,40,1024]{2,1,0:T(8,128)(2,1)}), bf16[16,40,1024]{2,1,0:T(8,128)(2,1)S(1)}, u32[]{:S(2)}, u32[]{:S(2)}) async-start(bf16[16,40,1024]{2,1,0:T(8,128)(2,1)} %bitcast.5), calls=%async_computation | async-start | bytes 2621440 | tf_op jit(solution)/shard_map/all_to_all | solution.py:165
  42.8 1.4 %copy-start.2 = (bf16[1,2048,384]{2,1,0:T(8,128)(2,1)S(1)}, bf16[1,2048,384]{2,1,0:T(8,128)(2,1)}, u32[]{:S(2)}) copy-start(bf16[1,2048,384]{2,1,0:T(8,128)(2,1)} %param.10) | copy-start | bytes 4718596
  44.2 1.4 %copy-start.3 = (bf16[1,2048,384]{2,1,0:T(8,128)(2,1)S(1)}, bf16[1,2048,384]{2,1,0:T(8,128)(2,1)}, u32[]{:S(2)}) copy-start(bf16[1,2048,384]{2,1,0:T(8,128)(2,1)} %param.11) | copy-start | bytes 4718596
  45.6 1.4 %copy-start.4 = (bf16[1,384,2048]{2,1,0:T(8,128)(2,1)S(1)}, bf16[1,384,2048]{2,1,0:T(8,128)(2,1)}, u32[]{:S(2)}) copy-start(bf16[1,384,2048]{2,1,0:T(8,128)(2,1)} %param.12) | copy-start | bytes 4718596
  53.6 1.1 copy-start.5
  54.7 0.9 copy-start.10
  55.6 70.9 %all-to-all-start.1 = ((bf16[16,40,1024]{2,1,0:T(8,128)(2,1)}), bf16[16,40,1024]{2,1,0:T(8,128)(2,1)S(1)}, u32[]{:S(2)}, u32[]{:S(2)}) async-start(bf16[16,40,1024]{2,1,0:T(8,128)(2,1)} %bitcast.20), calls=%async_computation.1 | async-start | bytes 2621440 | tf_op jit(solution)/shard_map/all_to_all | solution.py:184
  64.3 6.5 %collective-permute-start = (bf16[8,3,8,2048]{3,2,1,0:T(8,128)(2,1)}, bf16[8,3,8,2048]{3,2,1,0:T(8,128)(2,1)S(1)}, u32[]{:S(2)}, u32[]{:S(2)}) collective-permute-start(bf16[8,3,8,2048]{3,2,1,0:T(8,128)(2,1)} %copy-done.10), channel_id=1, source_target_pairs={{0,16},{16,0},{1,17},{17,1},{2,18},{18,2},{3,19},{19,3},{4,20},{20... | collective-permute-start | bytes 2359304 | tf_op jit(solution)/shard_map/ppermute | solution.py:187
  70.8 55.7 %copy-start.1 = (bf16[128,2048]{1,0:T(8,128)(2,1)S(1)}, bf16[128,2048]{1,0:T(8,128)(2,1)}, u32[]{:S(2)}) copy-start(bf16[128,2048]{1,0:T(8,128)(2,1)} %cot_ref.3) | copy-start | bytes 1572868
  70.8 55.7 %copy-start.8 = (f32[128,1]{0,1:T(1,128)S(1)}, f32[128,1]{0,1:T(1,128)}, u32[]{:S(2)}) copy-start(f32[128,1]{0,1:T(1,128)} %param.9) | copy-start | bytes 1540
  71.0 20.5 %collective-permute-start.1 = (bf16[3,8,2048]{2,1,0:T(8,128)(2,1)S(1)}, bf16[3,8,2048]{2,1,0:T(8,128)(2,1)S(1)}, u32[]{:S(2)}, u32[]{:S(2)}) collective-permute-start(bf16[3,8,2048]{2,1,0:T(8,128)(2,1)S(1)} %get-tuple-element.32), channel_id=1, source_target_pairs={{0,32},{32,64},{64,96},{96,128},{128,160},{160,192},{192,224},{224... | collective-permute-start | bytes 294920 | tf_op jit(solution)/shard_map/ppermute | solution.py:198
  74.2 22.3 %collective-permute-start.2 = (bf16[3,8,2048]{2,1,0:T(8,128)(2,1)S(1)}, bf16[3,8,2048]{2,1,0:T(8,128)(2,1)S(1)}, u32[]{:S(2)}, u32[]{:S(2)}) collective-permute-start(bf16[3,8,2048]{2,1,0:T(8,128)(2,1)S(1)} %get-tuple-element.33), channel_id=1, source_target_pairs={{0,64},{32,96},{64,128},{96,160},{128,192},{160,224},{192,0},{224,... | collective-permute-start | bytes 294920 | tf_op jit(solution)/shard_map/ppermute | solution.py:198
  78.4 21.1 %collective-permute-start.3 = (bf16[3,8,2048]{2,1,0:T(8,128)(2,1)S(1)}, bf16[3,8,2048]{2,1,0:T(8,128)(2,1)S(1)}, u32[]{:S(2)}, u32[]{:S(2)}) collective-permute-start(bf16[3,8,2048]{2,1,0:T(8,128)(2,1)S(1)} %get-tuple-element.34), channel_id=1, source_target_pairs={{0,96},{32,128},{64,160},{96,192},{128,224},{160,0},{192,32},{224,... | collective-permute-start | bytes 294920 | tf_op jit(solution)/shard_map/ppermute | solution.py:198
  83.1 16.4 %collective-permute-start.4 = (bf16[3,8,2048]{2,1,0:T(8,128)(2,1)S(1)}, bf16[3,8,2048]{2,1,0:T(8,128)(2,1)S(1)}, u32[]{:S(2)}, u32[]{:S(2)}) collective-permute-start(bf16[3,8,2048]{2,1,0:T(8,128)(2,1)S(1)} %get-tuple-element.35), channel_id=1, source_target_pairs={{0,128},{32,160},{64,192},{96,224},{128,0},{160,32},{192,64},{224,... | collective-permute-start | bytes 294920 | tf_op jit(solution)/shard_map/ppermute | solution.py:198
  86.6 12.9 %collective-permute-start.5 = (bf16[3,8,2048]{2,1,0:T(8,128)(2,1)S(1)}, bf16[3,8,2048]{2,1,0:T(8,128)(2,1)S(1)}, u32[]{:S(2)}, u32[]{:S(2)}) collective-permute-start(bf16[3,8,2048]{2,1,0:T(8,128)(2,1)S(1)} %get-tuple-element.36), channel_id=1, source_target_pairs={{0,160},{32,192},{64,224},{96,0},{128,32},{160,64},{192,96},{224,1... | collective-permute-start | bytes 294920 | tf_op jit(solution)/shard_map/ppermute | solution.py:198
  91.5 14.2 %collective-permute-start.6 = (bf16[3,8,2048]{2,1,0:T(8,128)(2,1)S(1)}, bf16[3,8,2048]{2,1,0:T(8,128)(2,1)S(1)}, u32[]{:S(2)}, u32[]{:S(2)}) collective-permute-start(bf16[3,8,2048]{2,1,0:T(8,128)(2,1)S(1)} %get-tuple-element.37), channel_id=1, source_target_pairs={{0,192},{32,224},{64,0},{96,32},{128,64},{160,96},{192,128},{224,1... | collective-permute-start | bytes 294920 | tf_op jit(solution)/shard_map/ppermute | solution.py:198
  96.5 10.2 %collective-permute-start.7 = (bf16[3,8,2048]{2,1,0:T(8,128)(2,1)S(1)}, bf16[3,8,2048]{2,1,0:T(8,128)(2,1)S(1)}, u32[]{:S(2)}, u32[]{:S(2)}) collective-permute-start(bf16[3,8,2048]{2,1,0:T(8,128)(2,1)S(1)} %get-tuple-element.38), channel_id=1, source_target_pairs={{0,224},{32,0},{64,32},{96,64},{128,96},{160,128},{192,160},{224,1... | collective-permute-start | bytes 294920 | tf_op jit(solution)/shard_map/ppermute | solution.py:198
  106.9 13.5 %collective-permute-start.8 = (bf16[8,2048]{1,0:T(8,128)(2,1)S(1)}, bf16[8,2048]{1,0:T(8,128)(2,1)S(1)}, u32[]{:S(2)}, u32[]{:S(2)}) collective-permute-start(bf16[8,2048]{1,0:T(8,128)(2,1)S(1)} %get-tuple-element.40), channel_id=1, source_target_pairs={{0,256},{256,512},{512,0},{1,257},{257,513},{513,1},{2,258},{258,5... | collective-permute-start | bytes 98312 | tf_op jit(solution)/shard_map/ppermute | solution.py:211
  117.2 8.7 %collective-permute-start.9 = (bf16[8,2048]{1,0:T(8,128)(2,1)S(1)}, bf16[8,2048]{1,0:T(8,128)(2,1)S(1)}, u32[]{:S(2)}, u32[]{:S(2)}) collective-permute-start(bf16[8,2048]{1,0:T(8,128)(2,1)S(1)} %get-tuple-element.41), channel_id=1, source_target_pairs={{0,512},{256,0},{512,256},{1,513},{257,1},{513,257},{2,514},{258,2... | collective-permute-start | bytes 98312 | tf_op jit(solution)/shard_map/ppermute | solution.py:211

commit v2 on v0

v2 whole, which is shorter than its diff:
```python
import functools
import math

import jax
import jax.numpy as jnp
from jax import lax
from jax.experimental import pallas as pl
from jax.experimental.pallas import tpu as pltpu
from jax.sharding import Mesh
from jax.sharding import PartitionSpec as P

BF = jnp.bfloat16
F32 = jnp.float32
DP = ("zhi", "y", "core")
EXPERT = ("zlo", "x")
EVERY = DP + EXPERT
VMEM_BYTES = 16 * 1024 * 1024
MAIN = 8
PARTS = 4


def dot(a, b, ca=1, cb=0):
    return lax.dot_general(a, b, (((ca,), (cb,)), ((), ())), preferred_element_type=F32)


def iota(shape, axis):
    return lax.broadcasted_iota(jnp.int32, shape, axis)


def where_bf(cond):
    return jnp.where(cond, 1.0, 0.0).astype(BF)


def picks(row, count):
    return where_bf(iota((count, row.shape[1]), 0) == row)


def column(row):
    n = row.shape[1]
    return jnp.sum(
        jnp.where(iota((n, n), 0) == iota((n, n), 1), row, jnp.zeros((), row.dtype)),
        axis=1,
        keepdims=True,
    )


def move(src, dst, sem):
    copy = pltpu.make_async_copy(src, dst, sem)
    copy.start()
    return copy


def dispatch_kernel(
    experts, routes_ref, gates_ref, tok_ref, cot_ref, send_ref, rows_ref, tok, cot, made, sem
):
    tokens, width = tok.shape
    half = width // 2
    first = move(tok_ref, tok, sem.at[0])
    second = move(cot_ref, cot, sem.at[1])
    routes = routes_ref[...]
    named = iota((experts, tokens), 0) == routes
    earlier = dot(
        where_bf(named), where_bf(iota((tokens, tokens), 0) < iota((tokens, tokens), 1))
    )
    slot = jnp.sum(jnp.where(named, earlier, 0.0), axis=0, keepdims=True).astype(jnp.int32)
    straight = jnp.where(slot < MAIN, routes * MAIN + slot, -1)
    folded = jnp.where(slot < MAIN, -PARTS, routes * MAIN + (slot - MAIN) * PARTS)
    rows_ref[...] = jnp.where(iota(rows_ref.shape, 0) == 0, straight, folded)
    gate = column(gates_ref[...])
    slots = send_ref.shape[0]
    pick = picks(straight, slots)
    fold = jnp.concatenate([picks(folded + part, slots) for part in range(PARTS)], axis=1)
    spans = [pl.ds(0, width), pl.ds(width, width), pl.ds(2 * width, half)]
    first.wait()
    plain = tok[...]
    made[:, :width] = dot(pick, plain).astype(BF)
    out = [move(made.at[:, spans[0]], send_ref.at[:, spans[0]], sem.at[2])]
    second.wait()
    graded = (gate * cot[...].astype(F32)).astype(BF)
    made[:, width : 2 * width] = dot(pick, graded).astype(BF)
    out.append(move(made.at[:, spans[1]], send_ref.at[:, spans[1]], sem.at[3]))
    sources = jnp.concatenate(
        [plain[:, :half], plain[:, half:], graded[:, :half], graded[:, half:]], axis=0
    )
    made[:, 2 * width :] = dot(fold, sources).astype(BF)
    out.append(move(made.at[:, spans[2]], send_ref.at[:, spans[2]], sem.at[4]))
    for copy in out:
        copy.wait()


def unfold(ranks, spare, part):
    shape = (ranks * spare, ranks * MAIN)
    r, q = iota(shape, 0), iota(shape, 1)
    return where_bf(q == (r // spare) * MAIN + (r % spare) * PARTS + part)


def product(hidden, grads, place_ref, blocks, own, scale):
    zhi, y, core = place_ref[0], place_ref[1], place_ref[2]
    sides, steps, line, depth, _ = blocks
    ring = sides * steps
    shape = (hidden.shape[1], sides * steps * line * depth)
    want = iota(shape, 1)
    side, rest = want // (steps * line * depth), want % (steps * line * depth)
    m, rest = rest // (line * depth), rest % (line * depth)
    j, row = rest // depth, rest % depth
    at = jnp.where(side == 0, y, lax.bitwise_xor(y, 1)) + 2 * m
    at = jnp.where(at >= ring, at - ring, at)
    up = zhi + j
    up = jnp.where(up >= line, up - line, up)
    chosen = core if own else 1 - core
    source = ((up * ring + at) * 2 + chosen) * depth + row
    ordered = dot(hidden, where_bf(iota(shape, 0) == source)).astype(BF)
    return (dot(ordered, grads, 0, 0) * scale).reshape(blocks)


def forward_kernel(
    ranks, spare, scale, place_ref, got_ref, wg_ref, wu_ref, give_ref, grad_ref, gate_ref, up_ref
):
    width = grad_ref.shape[1]
    fold = got_ref[:, 2 * width :]
    extra = [dot(unfold(ranks, spare, part), fold).astype(BF) for part in range(PARTS)]
    x = jnp.concatenate(
        [got_ref[:, :width], jnp.concatenate([extra[0], extra[1]], axis=1)], axis=0
    )
    g = jnp.concatenate(
        [got_ref[:, width : 2 * width], jnp.concatenate([extra[2], extra[3]], axis=1)], axis=0
    )
    grad_ref[...] = g
    pre_gate = dot(x, wg_ref[...])
    gate_ref[...] = pre_gate
    pre_up = dot(x, wu_ref[...])
    up_ref[...] = pre_up
    hidden = (pre_gate * jax.nn.sigmoid(pre_gate) * pre_up).astype(BF)
    give_ref[...] = product(hidden, g, place_ref, give_ref.shape, False, scale).astype(BF)


def backward_kernel(
    ranks, spare, scale, place_ref, grad_ref, gate_ref, up_ref, wd_ref, wg_ref, wu_ref,
    back_ref, keep_ref, made, wg, wu, sem,
):
    width = grad_ref.shape[1]
    half = width // 2
    straight = ranks * MAIN
    spans = [pl.ds(0, width), pl.ds(width, width), pl.ds(2 * width, half)]
    loads = [move(wg_ref, wg, sem.at[0]), move(wu_ref, wu, sem.at[1])]
    pre_gate, pre_up = gate_ref[...], up_ref[...]
    s = jax.nn.sigmoid(pre_gate)
    hidden = (pre_gate * s * pre_up).astype(BF)
    out = dot(hidden, wd_ref[...]).astype(BF)
    made[:, :width] = out[:straight]
    sent = [move(made.at[:, spans[0]], back_ref.at[:, spans[0]], sem.at[2])]
    grads = grad_ref[...]
    grad_hidden = dot(grads, wd_ref[...], 1, 1)
    grad_gate = (grad_hidden * pre_up * s * (1.0 + pre_gate * (1.0 - s))).astype(BF)
    grad_up = (grad_hidden * pre_gate * s).astype(BF)
    for load in loads:
        load.wait()
    grad_in = (dot(grad_gate, wg[...], 1, 1) + dot(grad_up, wu[...], 1, 1)).astype(BF)
    made[:, width : 2 * width] = grad_in[:straight]
    sent.append(move(made.at[:, spans[1]], back_ref.at[:, spans[1]], sem.at[3]))
    pieces = [out[straight:, :half], out[straight:, half:]]
    pieces += [grad_in[straight:, :half], grad_in[straight:, half:]]
    fold = [dot(unfold(ranks, spare, part), piece, 0, 0) for part, piece in enumerate(pieces)]
    made[:, 2 * width :] = (fold[0] + fold[1] + fold[2] + fold[3]).astype(BF)
    sent.append(move(made.at[:, spans[2]], back_ref.at[:, spans[2]], sem.at[4]))
    keep_ref[...] = product(hidden, grads, place_ref, keep_ref.shape, True, scale)
    for copy in sent:
        copy.wait()


def collect_kernel(rows_ref, gates_ref, cot_ref, back_ref, mixed_ref, dtok_ref, dgate_ref):
    tokens, width = cot_ref.shape
    half = width // 2
    slots = back_ref.shape[0]
    pick = picks(rows_ref[0:1, :], slots)
    folded = rows_ref[1:2, :]
    gate = column(gates_ref[...])
    inner = jnp.zeros((tokens, 1), F32)
    for part in range(PARTS):
        lanes = slice(part * half, (part + 1) * half)
        taken = dot(pick, back_ref[:, lanes], 0, 0)
        taken += dot(picks(folded + part, slots), back_ref[:, 2 * width :], 0, 0)
        if part < 2:
            mixed_ref[:, lanes] = (gate * taken).astype(BF)
            inner += jnp.sum(cot_ref[:, lanes].astype(F32) * taken, axis=1, keepdims=True)
        else:
            dtok_ref[:, part * half - width : (part + 1) * half - width] = taken.astype(BF)
    same = iota((tokens, tokens), 0) == iota((tokens, tokens), 1)
    dgate_ref[...] = jnp.sum(jnp.where(same, inner, 0.0), axis=0, keepdims=True)


def tree(parts):
    terms = [part.astype(F32) for part in parts]
    while len(terms) > 1:
        terms = [sum(terms[i : i + 2][1:], terms[i]) for i in range(0, len(terms), 2)]
    return terms[0]


def core_sum_kernel(keep_ref, other_ref, own_ref, give_ref):
    own_ref[...] = keep_ref[0] + other_ref[0].astype(F32)
    give_ref[...] = (keep_ref[1] + other_ref[1].astype(F32)).astype(BF)


def side_sum_kernel(own_ref, came_ref, *refs):
    for m, ref in enumerate(refs):
        ref[...] = (own_ref[m] + came_ref[m].astype(F32)).astype(ref.dtype)


def ring_sum_kernel(*refs):
    line = refs[0].shape[0]
    terms, sums = refs[: len(refs) - line], refs[len(refs) - line :]
    for j, ref in enumerate(sums):
        ref[...] = tree([term[j] for term in terms]).astype(ref.dtype)


def vmem(count):
    return [pl.BlockSpec(memory_space=pltpu.VMEM)] * count


def local(kernel, inputs, outputs, in_specs=None, out_specs=None, flops=0, **extra):
    return pl.pallas_call(
        kernel,
        out_shape=tuple(outputs),
        in_specs=in_specs or vmem(len(inputs)),
        out_specs=tuple(out_specs or vmem(len(outputs))),
        compiler_params=pltpu.CompilerParams(vmem_limit_bytes=VMEM_BYTES),
        cost_estimate=pl.CostEstimate(flops=flops, bytes_accessed=1 << 20, transcendentals=0),
        **extra,
    )(*inputs)


def onchip(x):
    return pltpu.with_memory_space_constraint(x, pltpu.VMEM)


def shaped(shape, dtype):
    return jax.ShapeDtypeStruct(shape, dtype)


def exchange_groups(zhi, ring, cores, zlo, xs):
    groups = []
    for core in range(cores):
        for window in range(zhi):
            for y in range(ring):
                group = []
                for z in range(zlo):
                    at = window if core == 0 or z >= zlo // 2 else (window + 1) % zhi
                    group += [(((at * ring + y) * cores + core) * zlo + z) * xs + x for x in range(xs)]
                groups.append(group)
    return groups


def per_device(tokens, routes, route_gates, w_gate, w_up, w_down, cotangent):
    rows, width = tokens.shape
    ranks = lax.axis_size(EXPERT)
    ff = w_gate.shape[2]
    zhi, ring, cores = (lax.axis_size(a) for a in DP)
    dp = zhi * ring * cores
    cap = 5 * rows * routes.shape[1] // (4 * ranks)
    spare = cap - MAIN
    lanes = 2 * width + width // 2
    groups = exchange_groups(zhi, ring, cores, *(lax.axis_size(a) for a in EXPERT))

    def exchange(values):
        return lax.all_to_all(
            values.reshape(ranks, MAIN, lanes),
            EVERY,
            split_axis=0,
            concat_axis=0,
            axis_index_groups=groups,
            tiled=True,
        ).reshape(ranks * MAIN, lanes)

    route_row = routes.reshape(1, rows)
    gate_row = route_gates.reshape(1, rows)
    far_off = pl.BlockSpec(memory_space=pltpu.HBM)
    anywhere = pl.BlockSpec(memory_space=pl.ANY)
    scalars = pl.BlockSpec(memory_space=pltpu.SMEM)
    slots = ranks * MAIN
    send, base = pl.pallas_call(
        functools.partial(dispatch_kernel, ranks),
        out_shape=(pltpu.HBM((slots, lanes), BF), shaped((8, rows), jnp.int32)),
        in_specs=vmem(2) + [anywhere] * 2,
        out_specs=(far_off, vmem(1)[0]),
        scratch_shapes=[
            pltpu.VMEM((rows, width), BF),
            pltpu.VMEM((rows, width), BF),
            pltpu.VMEM((slots, lanes), BF),
            pltpu.SemaphoreType.DMA((5,)),
        ],
        name="dispatch",
    )(route_row, gate_row, tokens, cotangent)
    got = exchange(send)
    depth = ff // dp
    scale = 1.0 / math.sqrt(routes.shape[1] * rows * dp)
    place = jnp.stack([lax.axis_index(a) for a in DP]).astype(jnp.int32)
    blocks = (2, ring // 2, zhi, depth, width)
    staged = [pltpu.VMEM((width, ff), BF), pltpu.VMEM((width, ff), BF)]
    give, grads, pre_gate, pre_up = local(
        functools.partial(forward_kernel, ranks, spare, scale),
        (place, onchip(got), w_gate[0], w_up[0]),
        [
            pltpu.VMEM(blocks, BF),
            pltpu.VMEM((ranks * cap, width), BF),
            pltpu.VMEM((ranks * cap, ff), F32),
            pltpu.VMEM((ranks * cap, ff), F32),
        ],
        in_specs=[scalars] + vmem(3),
        flops=6 * ranks * cap * ff * width,
    )
    other = lax.ppermute(give, "core", [(i, cores - 1 - i) for i in range(cores)])
    back, keep = local(
        functools.partial(backward_kernel, ranks, spare, scale),
        (place, grads, pre_gate, pre_up, w_down[0], w_gate[0], w_up[0]),
        [pltpu.HBM((slots, lanes), BF), pltpu.VMEM(blocks, F32)],
        in_specs=[scalars] + vmem(4) + [anywhere] * 2,
        out_specs=[far_off, vmem(1)[0]],
        flops=10 * ranks * cap * ff * width,
        scratch_shapes=[pltpu.VMEM((slots, lanes), BF)] + staged + [pltpu.SemaphoreType.DMA((5,))],
    )
    returned = exchange(back)
    own, side = local(
        core_sum_kernel,
        (keep, onchip(other)),
        [pltpu.VMEM(blocks[1:], F32), pltpu.VMEM(blocks[1:], BF)],
    )
    came = lax.ppermute(side, "y", [(i, i ^ 1) for i in range(ring)])
    steps = local(
        side_sum_kernel,
        (own, onchip(came)),
        [pltpu.VMEM(blocks[2:], BF if m else F32) for m in range(ring // 2)],
    )
    far = [
        lax.ppermute(steps[m], "y", [(i, (i + 2 * m) % ring) for i in range(ring)])
        for m in range(1, ring // 2)
    ]
    lines = local(
        ring_sum_kernel,
        (steps[0], *[onchip(f) for f in far]),
        [pltpu.VMEM(blocks[3:], BF if j else F32) for j in range(zhi)],
    )
    last = [
        lax.ppermute(lines[j], "zhi", [(i, (i + j) % zhi) for i in range(zhi)])
        for j in range(1, zhi)
    ]
    d_w_down = tree([lines[0], *last]).astype(BF)[None]
    mixed, d_tokens, d_gates = local(
        collect_kernel,
        (base, gate_row, cotangent, onchip(returned)),
        [shaped((rows, width), BF), shaped((rows, width), BF), shaped((1, rows), F32)],
    )
    return (mixed, d_tokens, d_gates.reshape(rows, 1), d_w_down)


def physical(mesh):
    dp, expert = (mesh.shape[a] for a in ("dp", "expert"))
    return Mesh(mesh.devices.reshape(3, dp // 6, 2, 4, expert // 4), EVERY)


def solution(mesh):
    every = P(EVERY, None)
    weight = P(EXPERT, None, None)
    return jax.shard_map(
        per_device,
        mesh=physical(mesh),
        in_specs=(every, every, every, weight, weight, weight, every),
        out_specs=(every, every, every, P(EXPERT, DP, None)),
        check_vma=False,
    )
```

time: 341 us -> 116 us (0.34)
  waiting for transfers between devices: 197 us -> 44.9 us
  blocking collectives: 96.2 us -> 0 us
  starting transfers between devices: 5.59 us -> 52.6 us
  between operations: 14.3 us -> 0.82 us
  Pallas kernels: 0 us -> 13.3 us
  local copies, waits for them, and re-layouts: 14.2 us -> 2.09 us
  matrix products: 6.5 us -> 0 us
  other arithmetic: 7.13 us -> 0.71 us
    reduce_scatter x1 -> x0, waiting for transfers between devices: 175 us -> none  [per_device(): lax.psum_scatter(product * grad_scale, 'dp', scatter_dimension=0, tiled=T...]
    all_to_all x3 -> x0, blocking collectives: 96.2 us -> none  [the longest x1 34.5 us: per_device(): lax.all_to_all(outgoing, 'expert', split_axis=0, concat_axis=0, tiled=True)]
    ppermute x0 -> x7, starting transfers between devices: none -> 28.6 us  [the longest x3 14.6 us: per_device(): lax.ppermute(steps[m], 'y', [(i, (i + 2 * m) % ring) for i in range(ring)])]
    ppermute x0 -> x7, waiting for transfers between devices: none -> 20.6 us  [the longest x1 9.5 us: per_device(): came = lax.ppermute(side, 'y', [(i, i ^ 1) for i in range(ring)])]
    all_to_all x1 -> x2, starting transfers between devices: 5.55 us -> 24 us  [exchange(): lax.all_to_all(values.reshape(ranks, MAIN, lanes), EVERY, split_axis=0, c...]
    pallas_call x0 -> x7, Pallas kernels: none -> 13.3 us  [the longest x6 9.33 us: local(): pl.pallas_call(kernel, out_shape=tuple(outputs), in_specs=in_specs or vme...]
    gather x6 -> x0, local copies, waits for them, and re-layouts: 6.91 us -> none  [the longest x2 3 us: per_device(): tokens[source_row // route_count]]
    dot_general x7 -> x0, matrix products: 6.5 us -> none  [the longest x1 2.41 us: per_device(): lax.dot_general(hidden_rows, grad_rows, (((0,), (0,)), ((), ())), preferr...]
  transfers between devices with their start and end apart: 2 -> 9, of which waited for: 2 -> 6; matrix products, arithmetic and copies ran while one was open for 1% -> 1% of each run, Pallas kernels for 0% -> 0%
where the time goes in v2:
time: 116 us; the launch traced here: 114 us
  starting transfers between devices  52.6 us (45%)
  waiting for transfers between devices  44.9 us (39%)
  Pallas kernels  13.3 us (11%)
  local copies, waits for them, and re-layouts  2.09 us (2%)
    all_to_all x2, waiting for transfers between devices, exchange(): lax.all_to_all(values.reshape(ranks, MAIN, lanes), EVERY, split_axis=0, c...  24.3 us
    all_to_all x2, starting transfers between devices, exchange(): lax.all_to_all(values.reshape(ranks, MAIN, lanes), EVERY, split_axis=0, c...  24 us
    ppermute x3, starting transfers between devices, per_device(): lax.ppermute(steps[m], 'y', [(i, (i + 2 * m) % ring) for i in range(ring)])  14.6 us
    ppermute x1, waiting for transfers between devices, per_device(): came = lax.ppermute(side, 'y', [(i, i ^ 1) for i in range(ring)])  9.5 us
    pallas_call x6, Pallas kernels, local(): pl.pallas_call(kernel, out_shape=tuple(outputs), in_specs=in_specs or vme...  9.33 us
    ppermute x2, starting transfers between devices, per_device(): lax.ppermute(lines[j], 'zhi', [(i, (i + j) % zhi) for i in range(zhi)])  9.19 us
    ppermute x3, waiting for transfers between devices, per_device(): lax.ppermute(steps[m], 'y', [(i, (i + 2 * m) % ring) for i in range(ring)])  5.89 us
    pallas_call x1, Pallas kernels, per_device(): pl.pallas_call(functools.partial(dispatch_kernel, ranks), out_shape=(pltp...  3.99 us
  transfers between devices with their start and end apart: 9, of which 6 were waited for; matrix products, arithmetic and copies ran while one was open for 1% of the time, Pallas kernels for 0%

profile of v2, /device:TPU:1, one launch (start us, length us, event | category | flops | bytes accessed | tf_op | source)
XLA Modules:
  0.0 114.5 jit_solution(4517472198841509248)
XLA Ops:
  0.6 0.0 copy-start.1
  0.6 4.0 %dispatch.1 = (bf16[128,5120]{1,0:T(8,128)(2,1)}, s32[8,128]{1,0:T(8,128)}) custom-call(s32[1,128]{1,0:T(1,128)} %bitcast.25, f32[1,128]{1,0:T(1,128)} %bitcast.21, bf16[128,2048]{1,0:T(8,128)(2,1)} %tok_ref.1, bf16[128,2048]{1,0:T(8,128)(2,1)} %cot_ref.3), custom_call_target="tpu_custom_call" | custom-call | tf_op jit(solution)/shard_map/dispatch/pallas_call | solution.py:280
  4.6 0.0 copy-start
  4.7 17.3 %all-to-all-start = ((bf16[16,8,5120]{2,1,0:T(8,128)(2,1)}), bf16[16,8,5120]{2,1,0:T(8,128)(2,1)}, u32[]{:S(2)}, u32[]{:S(2)}) async-start(bf16[16,8,5120]{2,1,0:T(8,128)(2,1)} %bitcast.24), calls=%async_computation | async-start | bytes 2621440 | tf_op jit(solution)/shard_map/all_to_all | solution.py:265
  21.9 0.1 pad_add_fusion.place_ref
  22.0 24.3 %all-to-all-done = bf16[16,8,5120]{2,1,0:T(8,128)(2,1)} async-done(((bf16[16,8,5120]{2,1,0:T(8,128)(2,1)}), bf16[16,8,5120]{2,1,0:T(8,128)(2,1)}, u32[]{:S(2)}, u32[]{:S(2)}) %all-to-all-start) | async-done | bytes 1310752 | tf_op jit(solution)/shard_map/all_to_all | solution.py:265
  46.3 0.0 copy-done
  46.3 3.0 %shard_map.102 = (bf16[2,4,3,8,2048]{4,3,2,1,0:T(8,128)(2,1)S(1)}, bf16[160,2048]{1,0:T(8,128)(2,1)S(1)}, f32[160,384]{1,0:T(8,128)S(1)}, f32[160,384]{1,0:T(8,128)S(1)}) custom-call(s32[3]{0:T(128)S(1)} %pad_add_fusion.place_ref, bf16[128,5120]{1,0:T(8,128)(2,1)} %bitcast.6.got_ref, bf16[2048,384]{1,0:T(8,128)(2,1)S(1)} %bitcast.15, ...), custom_call_target="tpu_custom_call" | custom-call | flops 754974720 | bytes 1048576 | tf_op jit(solution)/shard_map/pallas_call | solution.py:221
  49.4 0.9 copy-done.8
  50.2 0.0 copy-done.5
  50.2 4.4 %shard_map.103 = (bf16[128,5120]{1,0:T(8,128)(2,1)}, f32[2,4,3,8,2048]{4,3,2,1,0:T(8,128)S(1)}) custom-call(s32[3]{0:T(128)S(1)} %pad_add_fusion.place_ref, bf16[160,2048]{1,0:T(8,128)(2,1)S(1)} %get-tuple-element.26.grad_ref, f32[160,384]{1,0:T(8,128)S(1)} %get-tuple-element.27.gate_ref, f32[160,384]{1,0:T(8,128)S(1)} %get-tuple-element.28.up_ref, ...), custom_call_target="tpu_custom_call" | custom-call | flops 1258291200 | bytes 1048576 | tf_op jit(solution)/shard_map/pallas_call | solution.py:221
  54.7 1.2 %copy-done.3 = f32[2,4,3,8,2048]{4,3,2,1,0:T(8,128)} copy-done((f32[2,4,3,8,2048]{4,3,2,1,0:T(8,128)}, f32[2,4,3,8,2048]{4,3,2,1,0:T(8,128)S(1)}, u32[]{:S(2)}) %copy-start.3) | copy-done | bytes 1572888
  55.9 6.7 %all-to-all-start.1 = ((bf16[16,8,5120]{2,1,0:T(8,128)(2,1)}), bf16[16,8,5120]{2,1,0:T(8,128)(2,1)S(1)}, u32[]{:S(2)}, u32[]{:S(2)}) async-start(bf16[16,8,5120]{2,1,0:T(8,128)(2,1)} %bitcast.23), calls=%async_computation.1 | async-start | bytes 2621440 | tf_op jit(solution)/shard_map/all_to_all | solution.py:265
  62.6 1.9 %collective-permute-start = (bf16[2,4,3,8,2048]{4,3,2,1,0:T(8,128)(2,1)}, bf16[2,4,3,8,2048]{4,3,2,1,0:T(8,128)(2,1)S(1)}, u32[]{:S(2)}, u32[]{:S(2)}) collective-permute-start(bf16[2,4,3,8,2048]{4,3,2,1,0:T(8,128)(2,1)} %copy-done.8), channel_id=1, source_target_pairs={{0,16},{16,0},{1,17},{17,1},{2,18},{18,2},{3,19},{19,3},{4,20},{20... | collective-permute-start | bytes 2359304 | tf_op jit(solution)/shard_map/ppermute | solution.py:311
  64.5 2.5 %collective-permute-done.other_ref = bf16[2,4,3,8,2048]{4,3,2,1,0:T(8,128)(2,1)S(1)} collective-permute-done((bf16[2,4,3,8,2048]{4,3,2,1,0:T(8,128)(2,1)}, bf16[2,4,3,8,2048]{4,3,2,1,0:T(8,128)(2,1)S(1)}, u32[]{:S(2)}, u32[]{:S(2)}) %collective-permute-start) | collective-permute-done | bytes 786464 | tf_op jit(solution)/shard_map/ppermute | solution.py:311
  67.0 0.2 shard_map.105
  67.2 2.9 %collective-permute-start.1 = (bf16[4,3,8,2048]{3,2,1,0:T(8,128)(2,1)S(1)}, bf16[4,3,8,2048]{3,2,1,0:T(8,128)(2,1)S(1)}, u32[]{:S(2)}, u32[]{:S(2)}) collective-permute-start(bf16[4,3,8,2048]{3,2,1,0:T(8,128)(2,1)S(1)} %get-tuple-element.36), channel_id=1, source_target_pairs={{0,32},{32,0},{64,96},{96,64},{128,160},{160,128},{192,224},{224,1... | collective-permute-start | bytes 1179656 | tf_op jit(solution)/shard_map/ppermute | solution.py:327
  70.1 9.5 %collective-permute-done.1.came_ref = bf16[4,3,8,2048]{3,2,1,0:T(8,128)(2,1)S(1)} collective-permute-done((bf16[4,3,8,2048]{3,2,1,0:T(8,128)(2,1)S(1)}, bf16[4,3,8,2048]{3,2,1,0:T(8,128)(2,1)S(1)}, u32[]{:S(2)}, u32[]{:S(2)}) %collective-permute-start.1) | collective-permute-done | bytes 393248 | tf_op jit(solution)/shard_map/ppermute | solution.py:327
  79.6 0.1 shard_map.106
  79.7 3.9 %collective-permute-start.2 = (bf16[3,8,2048]{2,1,0:T(8,128)(2,1)S(1)}, bf16[3,8,2048]{2,1,0:T(8,128)(2,1)S(1)}, u32[]{:S(2)}, u32[]{:S(2)}) collective-permute-start(bf16[3,8,2048]{2,1,0:T(8,128)(2,1)S(1)} %get-tuple-element.38), channel_id=1, source_target_pairs={{0,64},{32,96},{64,128},{96,160},{128,192},{160,224},{192,0},{224,... | collective-permute-start | bytes 294920 | tf_op jit(solution)/shard_map/ppermute | solution.py:334
  83.6 5.7 %collective-permute-start.3 = (bf16[3,8,2048]{2,1,0:T(8,128)(2,1)S(1)}, bf16[3,8,2048]{2,1,0:T(8,128)(2,1)S(1)}, u32[]{:S(2)}, u32[]{:S(2)}) collective-permute-start(bf16[3,8,2048]{2,1,0:T(8,128)(2,1)S(1)} %get-tuple-element.39), channel_id=1, source_target_pairs={{0,128},{32,160},{64,192},{96,224},{128,0},{160,32},{192,64},{224,... | collective-permute-start | bytes 294920 | tf_op jit(solution)/shard_map/ppermute | solution.py:334
  89.3 5.0 %collective-permute-start.4 = (bf16[3,8,2048]{2,1,0:T(8,128)(2,1)S(1)}, bf16[3,8,2048]{2,1,0:T(8,128)(2,1)S(1)}, u32[]{:S(2)}, u32[]{:S(2)}) collective-permute-start(bf16[3,8,2048]{2,1,0:T(8,128)(2,1)S(1)} %get-tuple-element.40), channel_id=1, source_target_pairs={{0,192},{32,224},{64,0},{96,32},{128,64},{160,96},{192,128},{224,1... | collective-permute-start | bytes 294920 | tf_op jit(solution)/shard_map/ppermute | solution.py:334
  94.3 0.0 collective-permute-done.2.refs_1_
  94.3 1.1 collective-permute-done.3.refs_2_
  95.4 4.8 %collective-permute-done.4.refs_3_ = bf16[3,8,2048]{2,1,0:T(8,128)(2,1)S(1)} collective-permute-done((bf16[3,8,2048]{2,1,0:T(8,128)(2,1)S(1)}, bf16[3,8,2048]{2,1,0:T(8,128)(2,1)S(1)}, u32[]{:S(2)}, u32[]{:S(2)}) %collective-permute-start.4) | collective-permute-done | bytes 98336 | tf_op jit(solution)/shard_map/ppermute | solution.py:334
  100.3 3.3 %collective-permute-start.5 = (bf16[8,2048]{1,0:T(8,128)(2,1)S(1)}, bf16[8,2048]{1,0:T(8,128)(2,1)S(1)}, u32[]{:S(2)}, u32[]{:S(2)}) collective-permute-start(bf16[8,2048]{1,0:T(8,128)(2,1)S(1)} %get-tuple-element.42), channel_id=1, source_target_pairs={{0,256},{256,512},{512,0},{1,257},{257,513},{513,1},{2,258},{258,5... | collective-permute-start | bytes 98312 | tf_op jit(solution)/shard_map/ppermute | solution.py:343
  103.6 5.9 %collective-permute-start.6 = (bf16[8,2048]{1,0:T(8,128)(2,1)S(1)}, bf16[8,2048]{1,0:T(8,128)(2,1)S(1)}, u32[]{:S(2)}, u32[]{:S(2)}) collective-permute-start(bf16[8,2048]{1,0:T(8,128)(2,1)S(1)} %get-tuple-element.43), channel_id=1, source_target_pairs={{0,512},{256,0},{512,256},{1,513},{257,1},{513,257},{2,514},{258,2... | collective-permute-start | bytes 98312 | tf_op jit(solution)/shard_map/ppermute | solution.py:343
  109.5 0.0 collective-permute-done.5
  109.5 2.8 %collective-permute-done.6 = bf16[8,2048]{1,0:T(8,128)(2,1)S(1)} collective-permute-done((bf16[8,2048]{1,0:T(8,128)(2,1)S(1)}, bf16[8,2048]{1,0:T(8,128)(2,1)S(1)}, u32[]{:S(2)}, u32[]{:S(2)}) %collective-permute-start.6) | collective-permute-done | bytes 32800 | tf_op jit(solution)/shard_map/ppermute | solution.py:343
  112.2 0.6 fusion
  112.9 0.0 all-to-all-done.1
  112.9 1.6 %shard_map.104 = (bf16[128,2048]{1,0:T(8,128)(2,1)}, bf16[128,2048]{1,0:T(8,128)(2,1)}, f32[1,128]{1,0:T(1,128)}) custom-call(s32[8,128]{1,0:T(8,128)S(1)} %copy-done.6, f32[1,128]{1,0:T(1,128)S(1)} %bitcast.22, bf16[128,2048]{1,0:T(8,128)(2,1)S(1)} %copy-done.2, bf16[128,5120]{1,0:T(8,128)(2,1)S(1)} %bitcast.19), custom_call_target="tpu_custom_call" | custom-call | bytes 1048576 | tf_op jit(solution)/shard_map/pallas_call | solution.py:221
  (13 shorter events, 0.1 us)
Async XLA Ops:
  0.6 45.7 %copy-start.1 = (bf16[1,2048,384]{2,1,0:T(8,128)(2,1)S(1)}, bf16[1,2048,384]{2,1,0:T(8,128)(2,1)}, u32[]{:S(2)}) copy-start(bf16[1,2048,384]{2,1,0:T(8,128)(2,1)} %param.11) | copy-start | bytes 4718596
  4.6 41.7 %copy-start = (bf16[1,2048,384]{2,1,0:T(8,128)(2,1)S(1)}, bf16[1,2048,384]{2,1,0:T(8,128)(2,1)}, u32[]{:S(2)}) copy-start(bf16[1,2048,384]{2,1,0:T(8,128)(2,1)} %param.10) | copy-start | bytes 4718596
  4.7 41.6 %all-to-all-start = ((bf16[16,8,5120]{2,1,0:T(8,128)(2,1)}), bf16[16,8,5120]{2,1,0:T(8,128)(2,1)}, u32[]{:S(2)}, u32[]{:S(2)}) async-start(bf16[16,8,5120]{2,1,0:T(8,128)(2,1)} %bitcast.24), calls=%async_computation | async-start | bytes 2621440 | tf_op jit(solution)/shard_map/all_to_all | solution.py:265
  46.3 3.9 %copy-start.5 = (bf16[1,384,2048]{2,1,0:T(8,128)(2,1)S(1)}, bf16[1,384,2048]{2,1,0:T(8,128)(2,1)}, u32[]{:S(2)}) copy-start(bf16[1,384,2048]{2,1,0:T(8,128)(2,1)} %param.12) | copy-start | bytes 4718596
  49.3 0.9 copy-start.8
  54.7 1.2 %copy-start.3 = (f32[2,4,3,8,2048]{4,3,2,1,0:T(8,128)}, f32[2,4,3,8,2048]{4,3,2,1,0:T(8,128)S(1)}, u32[]{:S(2)}) copy-start(f32[2,4,3,8,2048]{4,3,2,1,0:T(8,128)S(1)} %get-tuple-element.33.keep_ref) | copy-start | bytes 4718596
  55.9 11.1 %copy-start.4 = (f32[2,4,3,8,2048]{4,3,2,1,0:T(8,128)S(1)}, f32[2,4,3,8,2048]{4,3,2,1,0:T(8,128)}, u32[]{:S(2)}) copy-start(f32[2,4,3,8,2048]{4,3,2,1,0:T(8,128)} %copy-done.3) | copy-start | bytes 4718596
  55.9 57.0 %all-to-all-start.1 = ((bf16[16,8,5120]{2,1,0:T(8,128)(2,1)}), bf16[16,8,5120]{2,1,0:T(8,128)(2,1)S(1)}, u32[]{:S(2)}, u32[]{:S(2)}) async-start(bf16[16,8,5120]{2,1,0:T(8,128)(2,1)} %bitcast.23), calls=%async_computation.1 | async-start | bytes 2621440 | tf_op jit(solution)/shard_map/all_to_all | solution.py:265
  62.6 4.4 %collective-permute-start = (bf16[2,4,3,8,2048]{4,3,2,1,0:T(8,128)(2,1)}, bf16[2,4,3,8,2048]{4,3,2,1,0:T(8,128)(2,1)S(1)}, u32[]{:S(2)}, u32[]{:S(2)}) collective-permute-start(bf16[2,4,3,8,2048]{4,3,2,1,0:T(8,128)(2,1)} %copy-done.8), channel_id=1, source_target_pairs={{0,16},{16,0},{1,17},{17,1},{2,18},{18,2},{3,19},{19,3},{4,20},{20... | collective-permute-start | bytes 2359304 | tf_op jit(solution)/shard_map/ppermute | solution.py:311
  67.0 45.9 %copy-start.2 = (bf16[128,2048]{1,0:T(8,128)(2,1)S(1)}, bf16[128,2048]{1,0:T(8,128)(2,1)}, u32[]{:S(2)}) copy-start(bf16[128,2048]{1,0:T(8,128)(2,1)} %cot_ref.3) | copy-start | bytes 1572868
  67.0 45.9 %copy-start.6 = (s32[8,128]{1,0:T(8,128)S(1)}, s32[8,128]{1,0:T(8,128)}, u32[]{:S(2)}) copy-start(s32[8,128]{1,0:T(8,128)} %get-tuple-element.24.rows_ref) | copy-start | bytes 12292
  67.0 45.9 %copy-start.7 = (f32[128,1]{0,1:T(1,128)S(1)}, f32[128,1]{0,1:T(1,128)}, u32[]{:S(2)}) copy-start(f32[128,1]{0,1:T(1,128)} %param.9) | copy-start | bytes 1540
  67.2 12.4 %collective-permute-start.1 = (bf16[4,3,8,2048]{3,2,1,0:T(8,128)(2,1)S(1)}, bf16[4,3,8,2048]{3,2,1,0:T(8,128)(2,1)S(1)}, u32[]{:S(2)}, u32[]{:S(2)}) collective-permute-start(bf16[4,3,8,2048]{3,2,1,0:T(8,128)(2,1)S(1)} %get-tuple-element.36), channel_id=1, source_target_pairs={{0,32},{32,0},{64,96},{96,64},{128,160},{160,128},{192,224},{224,1... | collective-permute-start | bytes 1179656 | tf_op jit(solution)/shard_map/ppermute | solution.py:327
  79.7 14.6 %collective-permute-start.2 = (bf16[3,8,2048]{2,1,0:T(8,128)(2,1)S(1)}, bf16[3,8,2048]{2,1,0:T(8,128)(2,1)S(1)}, u32[]{:S(2)}, u32[]{:S(2)}) collective-permute-start(bf16[3,8,2048]{2,1,0:T(8,128)(2,1)S(1)} %get-tuple-element.38), channel_id=1, source_target_pairs={{0,64},{32,96},{64,128},{96,160},{128,192},{160,224},{192,0},{224,... | collective-permute-start | bytes 294920 | tf_op jit(solution)/shard_map/ppermute | solution.py:334
  83.6 11.8 %collective-permute-start.3 = (bf16[3,8,2048]{2,1,0:T(8,128)(2,1)S(1)}, bf16[3,8,2048]{2,1,0:T(8,128)(2,1)S(1)}, u32[]{:S(2)}, u32[]{:S(2)}) collective-permute-start(bf16[3,8,2048]{2,1,0:T(8,128)(2,1)S(1)} %get-tuple-element.39), channel_id=1, source_target_pairs={{0,128},{32,160},{64,192},{96,224},{128,0},{160,32},{192,64},{224,... | collective-permute-start | bytes 294920 | tf_op jit(solution)/shard_map/ppermute | solution.py:334
  89.3 10.9 %collective-permute-start.4 = (bf16[3,8,2048]{2,1,0:T(8,128)(2,1)S(1)}, bf16[3,8,2048]{2,1,0:T(8,128)(2,1)S(1)}, u32[]{:S(2)}, u32[]{:S(2)}) collective-permute-start(bf16[3,8,2048]{2,1,0:T(8,128)(2,1)S(1)} %get-tuple-element.40), channel_id=1, source_target_pairs={{0,192},{32,224},{64,0},{96,32},{128,64},{160,96},{192,128},{224,1... | collective-permute-start | bytes 294920 | tf_op jit(solution)/shard_map/ppermute | solution.py:334
  100.3 9.2 %collective-permute-start.5 = (bf16[8,2048]{1,0:T(8,128)(2,1)S(1)}, bf16[8,2048]{1,0:T(8,128)(2,1)S(1)}, u32[]{:S(2)}, u32[]{:S(2)}) collective-permute-start(bf16[8,2048]{1,0:T(8,128)(2,1)S(1)} %get-tuple-element.42), channel_id=1, source_target_pairs={{0,256},{256,512},{512,0},{1,257},{257,513},{513,1},{2,258},{258,5... | collective-permute-start | bytes 98312 | tf_op jit(solution)/shard_map/ppermute | solution.py:343
  103.6 8.7 %collective-permute-start.6 = (bf16[8,2048]{1,0:T(8,128)(2,1)S(1)}, bf16[8,2048]{1,0:T(8,128)(2,1)S(1)}, u32[]{:S(2)}, u32[]{:S(2)}) collective-permute-start(bf16[8,2048]{1,0:T(8,128)(2,1)S(1)} %get-tuple-element.43), channel_id=1, source_target_pairs={{0,512},{256,0},{512,256},{1,513},{257,1},{513,257},{2,514},{258,2... | collective-permute-start | bytes 98312 | tf_op jit(solution)/shard_map/ppermute | solution.py:343

commit v3 on v2

--- a/solution.py
+++ b/solution.py
@@ -14,7 +14,7 @@
 DP = ("zhi", "y", "core")
 EXPERT = ("zlo", "x")
 EVERY = DP + EXPERT
-VMEM_BYTES = 16 * 1024 * 1024
+VMEM_BYTES = 24 * 1024 * 1024
 MAIN = 8
 PARTS = 4
 
@@ -51,12 +51,14 @@
 
 
 def dispatch_kernel(
-    experts, routes_ref, gates_ref, tok_ref, cot_ref, send_ref, rows_ref, tok, cot, made, sem
+    experts, routes_ref, gates_ref, tok_ref, cot_ref, send_ref, rows_ref, held, made, sem
 ):
-    tokens, width = tok.shape
-    half = width // 2
-    first = move(tok_ref, tok, sem.at[0])
-    second = move(cot_ref, cot, sem.at[1])
+    _, tokens, half = held.shape
+    loads = []
+    for part in range(PARTS):
+        lanes = pl.ds((part % 2) * half, half)
+        source = tok_ref if part < 2 else cot_ref
+        loads.append(move(source.at[:, lanes], held.at[part], sem.at[part]))
     routes = routes_ref[...]
     named = iota((experts, tokens), 0) == routes
     earlier = dot(
@@ -69,22 +71,24 @@
     gate = column(gates_ref[...])
     slots = send_ref.shape[0]
     pick = picks(straight, slots)
-    fold = jnp.concatenate([picks(folded + part, slots) for part in range(PARTS)], axis=1)
-    spans = [pl.ds(0, width), pl.ds(width, width), pl.ds(2 * width, half)]
-    first.wait()
-    plain = tok[...]
-    made[:, :width] = dot(pick, plain).astype(BF)
-    out = [move(made.at[:, spans[0]], send_ref.at[:, spans[0]], sem.at[2])]
-    second.wait()
-    graded = (gate * cot[...].astype(F32)).astype(BF)
-    made[:, width : 2 * width] = dot(pick, graded).astype(BF)
-    out.append(move(made.at[:, spans[1]], send_ref.at[:, spans[1]], sem.at[3]))
-    sources = jnp.concatenate(
-        [plain[:, :half], plain[:, half:], graded[:, :half], graded[:, half:]], axis=0
-    )
-    made[:, 2 * width :] = dot(fold, sources).astype(BF)
-    out.append(move(made.at[:, spans[2]], send_ref.at[:, spans[2]], sem.at[4]))
-    for copy in out:
+    stores = []
+
+    def store(part):
+        lanes = pl.ds(part * half, half)
+        stores.append(move(made.at[:, lanes], send_ref.at[:, lanes], sem.at[PARTS + part]))
+
+    fold = jnp.zeros((slots, half), F32)
+    for part in range(PARTS):
+        loads[part].wait()
+        value = held[part]
+        if part >= 2:
+            value = (gate * value.astype(F32)).astype(BF)
+        made[:, part * half : (part + 1) * half] = dot(pick, value).astype(BF)
+        store(part)
+        fold += dot(picks(folded + part, slots), value)
+    made[:, PARTS * half :] = fold.astype(BF)
+    store(PARTS)
+    for copy in stores:
         copy.wait()
 
 
@@ -94,13 +98,13 @@
     return where_bf(q == (r // spare) * MAIN + (r % spare) * PARTS + part)
 
 
-def product(hidden, grads, place_ref, blocks, own, scale):
+def product(hidden, grads, place_ref, shape, sides, own, scale):
     zhi, y, core = place_ref[0], place_ref[1], place_ref[2]
-    sides, steps, line, depth, _ = blocks
-    ring = sides * steps
-    shape = (hidden.shape[1], sides * steps * line * depth)
-    want = iota(shape, 1)
-    side, rest = want // (steps * line * depth), want % (steps * line * depth)
+    steps, line, depth, _ = shape[-4:]
+    ring = 2 * steps
+    spread = (hidden.shape[1], len(sides) * steps * line * depth)
+    want = iota(spread, 1)
+    side, rest = want // (steps * line * depth) + sides[0], want % (steps * line * depth)
     m, rest = rest // (line * depth), rest % (line * depth)
     j, row = rest // depth, rest % depth
     at = jnp.where(side == 0, y, lax.bitwise_xor(y, 1)) + 2 * m
@@ -109,48 +113,64 @@
     up = jnp.where(up >= line, up - line, up)
     chosen = core if own else 1 - core
     source = ((up * ring + at) * 2 + chosen) * depth + row
-    ordered = dot(hidden, where_bf(iota(shape, 0) == source)).astype(BF)
-    return (dot(ordered, grads, 0, 0) * scale).reshape(blocks)
+    ordered = dot(hidden, where_bf(iota(spread, 0) == source)).astype(BF)
+    return (dot(ordered, grads, 0, 0) * scale).reshape(shape)
 
 
 def forward_kernel(
-    ranks, spare, scale, place_ref, got_ref, wg_ref, wu_ref, give_ref, grad_ref, gate_ref, up_ref
+    ranks, spare, scale, place_ref, got_ref, wg_ref, wu_ref, give_ref, grad_ref, hidden_ref,
+    gate_ref, up_ref, held, sem,
 ):
     width = grad_ref.shape[1]
-    fold = got_ref[:, 2 * width :]
-    extra = [dot(unfold(ranks, spare, part), fold).astype(BF) for part in range(PARTS)]
-    x = jnp.concatenate(
-        [got_ref[:, :width], jnp.concatenate([extra[0], extra[1]], axis=1)], axis=0
-    )
-    g = jnp.concatenate(
-        [got_ref[:, width : 2 * width], jnp.concatenate([extra[2], extra[3]], axis=1)], axis=0
-    )
-    grad_ref[...] = g
+    straight = ranks * MAIN
+    spans = [pl.ds(2 * width, width // 2), pl.ds(0, width), pl.ds(width, width)]
+    loads = [move(got_ref.at[:, at], held.at[:, at], sem.at[i]) for i, at in enumerate(spans)]
+    pick = [unfold(ranks, spare, part) for part in range(PARTS)]
+    loads[0].wait()
+    fold = held[:, 2 * width :]
+    extra = [dot(pick[part], fold).astype(BF) for part in range(PARTS)]
+    grad_ref[straight:, :] = jnp.concatenate(extra[2:], axis=1)
+    loads[1].wait()
+    x = jnp.concatenate([held[:, :width], jnp.concatenate(extra[:2], axis=1)], axis=0)
     pre_gate = dot(x, wg_ref[...])
     gate_ref[...] = pre_gate
     pre_up = dot(x, wu_ref[...])
     up_ref[...] = pre_up
     hidden = (pre_gate * jax.nn.sigmoid(pre_gate) * pre_up).astype(BF)
-    give_ref[...] = product(hidden, g, place_ref, give_ref.shape, False, scale).astype(BF)
+    hidden_ref[...] = hidden
+    loads[2].wait()
+    grad_ref[:straight, :] = held[:, width : 2 * width]
+    give_ref[...] = product(
+        hidden, grad_ref[...], place_ref, give_ref.shape, (0, 1), False, scale
+    ).astype(BF)
+
+
+def core_sum_kernel(scale, place_ref, grad_ref, hidden_ref, other_ref, side_ref):
+    made = product(hidden_ref[...], grad_ref[...], place_ref, side_ref.shape, (1,), True, scale)
+    side_ref[...] = (made + other_ref[1].astype(F32)).astype(BF)
 
 
 def backward_kernel(
-    ranks, spare, scale, place_ref, grad_ref, gate_ref, up_ref, wd_ref, wg_ref, wu_ref,
-    back_ref, keep_ref, made, wg, wu, sem,
+    ranks, spare, scale, place_ref, grad_ref, hidden_ref, gate_ref, up_ref, wd_ref, wg_ref, wu_ref,
+    other_ref, back_ref, own_ref, made, kept, wd, wg, wu, sem,
 ):
     width = grad_ref.shape[1]
     half = width // 2
     straight = ranks * MAIN
     spans = [pl.ds(0, width), pl.ds(width, width), pl.ds(2 * width, half)]
+    first = move(wd_ref, wd, sem.at[5])
     loads = [move(wg_ref, wg, sem.at[0]), move(wu_ref, wu, sem.at[1])]
+    hidden, grads = hidden_ref[...], grad_ref[...]
+    mine = product(hidden, grads, place_ref, own_ref.shape, (0,), True, scale)
+    kept[...] = mine + other_ref[0].astype(F32)
+    sent = [move(kept, own_ref, sem.at[6])]
     pre_gate, pre_up = gate_ref[...], up_ref[...]
     s = jax.nn.sigmoid(pre_gate)
-    hidden = (pre_gate * s * pre_up).astype(BF)
-    out = dot(hidden, wd_ref[...]).astype(BF)
+    first.wait()
+    out = dot(hidden, wd[...]).astype(BF)
     made[:, :width] = out[:straight]
-    sent = [move(made.at[:, spans[0]], back_ref.at[:, spans[0]], sem.at[2])]
-    grads = grad_ref[...]
-    grad_hidden = dot(grads, wd_ref[...], 1, 1)
+    sent.append(move(made.at[:, spans[0]], back_ref.at[:, spans[0]], sem.at[2]))
+    grad_hidden = dot(grads, wd[...], 1, 1)
     grad_gate = (grad_hidden * pre_up * s * (1.0 + pre_gate * (1.0 - s))).astype(BF)
     grad_up = (grad_hidden * pre_gate * s).astype(BF)
     for load in loads:
@@ -163,7 +183,6 @@
     fold = [dot(unfold(ranks, spare, part), piece, 0, 0) for part, piece in enumerate(pieces)]
     made[:, 2 * width :] = (fold[0] + fold[1] + fold[2] + fold[3]).astype(BF)
     sent.append(move(made.at[:, spans[2]], back_ref.at[:, spans[2]], sem.at[4]))
-    keep_ref[...] = product(hidden, grads, place_ref, keep_ref.shape, True, scale)
     for copy in sent:
         copy.wait()
 
@@ -196,11 +215,6 @@
     return terms[0]
 
 
-def core_sum_kernel(keep_ref, other_ref, own_ref, give_ref):
-    own_ref[...] = keep_ref[0] + other_ref[0].astype(F32)
-    give_ref[...] = (keep_ref[1] + other_ref[1].astype(F32)).astype(BF)
-
-
 def side_sum_kernel(own_ref, came_ref, *refs):
     for m, ref in enumerate(refs):
         ref[...] = (own_ref[m] + came_ref[m].astype(F32)).astype(ref.dtype)
@@ -231,6 +245,10 @@
 
 def onchip(x):
     return pltpu.with_memory_space_constraint(x, pltpu.VMEM)
+
+
+def offchip(x):
+    return pltpu.with_memory_space_constraint(x, pltpu.HBM)
 
 
 def shaped(shape, dtype):
@@ -283,10 +301,9 @@
         in_specs=vmem(2) + [anywhere] * 2,
         out_specs=(far_off, vmem(1)[0]),
         scratch_shapes=[
-            pltpu.VMEM((rows, width), BF),
-            pltpu.VMEM((rows, width), BF),
+            pltpu.VMEM((PARTS, rows, width // 2), BF),
             pltpu.VMEM((slots, lanes), BF),
-            pltpu.SemaphoreType.DMA((5,)),
+            pltpu.SemaphoreType.DMA((2 * PARTS + 1,)),
         ],
         name="dispatch",
     )(route_row, gate_row, tokens, cotangent)
@@ -295,35 +312,42 @@
     scale = 1.0 / math.sqrt(routes.shape[1] * rows * dp)
     place = jnp.stack([lax.axis_index(a) for a in DP]).astype(jnp.int32)
     blocks = (2, ring // 2, zhi, depth, width)
-    staged = [pltpu.VMEM((width, ff), BF), pltpu.VMEM((width, ff), BF)]
-    give, grads, pre_gate, pre_up = local(
+    give, grads, hidden, pre_gate, pre_up = local(
         functools.partial(forward_kernel, ranks, spare, scale),
-        (place, onchip(got), w_gate[0], w_up[0]),
+        (place, got, w_gate[0], w_up[0]),
         [
             pltpu.VMEM(blocks, BF),
             pltpu.VMEM((ranks * cap, width), BF),
+            pltpu.VMEM((ranks * cap, ff), BF),
             pltpu.VMEM((ranks * cap, ff), F32),
             pltpu.VMEM((ranks * cap, ff), F32),
         ],
+        in_specs=[scalars, anywhere] + vmem(2),
+        flops=6 * ranks * cap * ff * width,
+        scratch_shapes=[pltpu.VMEM((slots, lanes), BF), pltpu.SemaphoreType.DMA((3,))],
+    )
+    other = lax.ppermute(give, "core", [(i, cores - 1 - i) for i in range(cores)])
+    (side,) = local(
+        functools.partial(core_sum_kernel, scale),
+        (place, grads, hidden, onchip(other)),
+        [pltpu.VMEM(blocks[1:], BF)],
         in_specs=[scalars] + vmem(3),
-        flops=6 * ranks * cap * ff * width,
-    )
-    other = lax.ppermute(give, "core", [(i, cores - 1 - i) for i in range(cores)])
-    back, keep = local(
+    )
+    back, own = local(
         functools.partial(backward_kernel, ranks, spare, scale),
-        (place, grads, pre_gate, pre_up, w_down[0], w_gate[0], w_up[0]),
-        [pltpu.HBM((slots, lanes), BF), pltpu.VMEM(blocks, F32)],
-        in_specs=[scalars] + vmem(4) + [anywhere] * 2,
-        out_specs=[far_off, vmem(1)[0]],
+        (place, grads, hidden, pre_gate, pre_up, *[offchip(w[0]) for w in (w_down, w_gate, w_up)], onchip(other)),
+        [pltpu.HBM((slots, lanes), BF), pltpu.HBM(blocks[1:], F32)],
+        in_specs=[scalars] + vmem(4) + [anywhere] * 3 + vmem(1),
+        out_specs=[far_off] * 2,
         flops=10 * ranks * cap * ff * width,
-        scratch_shapes=[pltpu.VMEM((slots, lanes), BF)] + staged + [pltpu.SemaphoreType.DMA((5,))],
+        scratch_shapes=[
+            pltpu.VMEM((slots, lanes), BF),
+            pltpu.VMEM(blocks[1:], F32),
+            *[pltpu.VMEM(w.shape[1:], BF) for w in (w_down, w_gate, w_up)],
+            pltpu.SemaphoreType.DMA((7,)),
+        ],
     )
     returned = exchange(back)
-    own, side = local(
-        core_sum_kernel,
-        (keep, onchip(other)),
-        [pltpu.VMEM(blocks[1:], F32), pltpu.VMEM(blocks[1:], BF)],
-    )
     came = lax.ppermute(side, "y", [(i, i ^ 1) for i in range(ring)])
     steps = local(
         side_sum_kernel,

time: 116 us -> 116 us (level)
  Pallas kernels: 13.3 us -> 16 us
  local copies, waits for them, and re-layouts: 2.09 us -> 0.04 us
    pallas_call x6, Pallas kernels: 9.33 us -> 11.8 us  [local(): pl.pallas_call(kernel, out_shape=tuple(outputs), in_specs=in_specs or vme...]
    unnamed x18 -> x16, local copies, waits for them, and re-layouts: 2.09 us -> 0.04 us
  transfers between devices with their start and end apart: 9 -> 9, of which waited for: 6 -> 6; matrix products, arithmetic and copies ran while one was open for 1% -> 1% of each run, Pallas kernels for 0% -> 1%
where the time goes in v3:
time: 116 us; the launch traced here: 115 us
  starting transfers between devices  52.7 us (45%)
  waiting for transfers between devices  44.7 us (39%)
  Pallas kernels  16 us (14%)
    all_to_all x2, waiting for transfers between devices, exchange(): lax.all_to_all(values.reshape(ranks, MAIN, lanes), EVERY, split_axis=0, c...  24.3 us
    all_to_all x2, starting transfers between devices, exchange(): lax.all_to_all(values.reshape(ranks, MAIN, lanes), EVERY, split_axis=0, c...  24 us
    ppermute x3, starting transfers between devices, per_device(): lax.ppermute(steps[m], 'y', [(i, (i + 2 * m) % ring) for i in range(ring)])  14.6 us
    pallas_call x6, Pallas kernels, local(): pl.pallas_call(kernel, out_shape=tuple(outputs), in_specs=in_specs or vme...  11.8 us
    ppermute x1, waiting for transfers between devices, per_device(): came = lax.ppermute(side, 'y', [(i, i ^ 1) for i in range(ring)])  9.26 us
    ppermute x2, starting transfers between devices, per_device(): lax.ppermute(lines[j], 'zhi', [(i, (i + j) % zhi) for i in range(zhi)])  9.19 us
    ppermute x3, waiting for transfers between devices, per_device(): lax.ppermute(steps[m], 'y', [(i, (i + 2 * m) % ring) for i in range(ring)])  6.09 us
    pallas_call x1, Pallas kernels, per_device(): pl.pallas_call(functools.partial(dispatch_kernel, ranks), out_shape=(pltp...  4.21 us
  transfers between devices with their start and end apart: 9, of which 6 were waited for; matrix products, arithmetic and copies ran while one was open for 1% of the time, Pallas kernels for 1%

profile of v3, /device:TPU:1, one launch (start us, length us, event | category | flops | bytes accessed | tf_op | source)
XLA Modules:
  0.0 115.0 jit_solution(17372967234082213161)
XLA Ops:
  0.6 0.0 copy-start.1
  0.6 4.2 %dispatch.1 = (bf16[128,5120]{1,0:T(8,128)(2,1)}, s32[8,128]{1,0:T(8,128)}) custom-call(s32[1,128]{1,0:T(1,128)} %bitcast.25, f32[1,128]{1,0:T(1,128)} %bitcast.20, bf16[128,2048]{1,0:T(8,128)(2,1)} %tok_ref.1, bf16[128,2048]{1,0:T(8,128)(2,1)} %cot_ref.3), custom_call_target="tpu_custom_call" | custom-call | tf_op jit(solution)/shard_map/dispatch/pallas_call | solution.py:298
  4.9 0.0 copy-start
  4.9 17.2 %all-to-all-start = ((bf16[16,8,5120]{2,1,0:T(8,128)(2,1)}), bf16[16,8,5120]{2,1,0:T(8,128)(2,1)}, u32[]{:S(2)}, u32[]{:S(2)}) async-start(bf16[16,8,5120]{2,1,0:T(8,128)(2,1)} %bitcast.24), calls=%async_computation | async-start | bytes 2621440 | tf_op jit(solution)/shard_map/all_to_all | solution.py:283
  22.1 0.1 pad_add_fusion.place_ref
  22.2 24.3 %all-to-all-done = bf16[16,8,5120]{2,1,0:T(8,128)(2,1)} async-done(((bf16[16,8,5120]{2,1,0:T(8,128)(2,1)}), bf16[16,8,5120]{2,1,0:T(8,128)(2,1)}, u32[]{:S(2)}, u32[]{:S(2)}) %all-to-all-start) | async-done | bytes 1310752 | tf_op jit(solution)/shard_map/all_to_all | solution.py:283
  46.5 3.4 %shard_map.102 = (bf16[2,4,3,8,2048]{4,3,2,1,0:T(8,128)(2,1)S(1)}, bf16[160,2048]{1,0:T(8,128)(2,1)S(1)}, bf16[160,384]{1,0:T(8,128)(2,1)S(1)}, f32[160,384]{1,0:T(8,128)S(1)}, f32[160,384]{1,0:T(8,128)S(1)}) custom-call(s32[3]{0:T(128)S(1)} %pad_add_fusion.place_ref, bf16[128,5120]{1,0:T(8,128)(2,1)} %bitcast.6.got_ref, bf16[2048,384]{1,0:T(8,128)(2,1)S(1)} %bitcast.16, ...), custom_call_target="tpu_custom_call" | custom-call | flops 754974720 | bytes 1048576 | tf_op jit(solution)/shard_map/pallas_call | solution.py:235
  49.9 1.9 %collective-permute-start = (bf16[2,4,3,8,2048]{4,3,2,1,0:T(8,128)(2,1)S(1)}, bf16[2,4,3,8,2048]{4,3,2,1,0:T(8,128)(2,1)S(1)}, u32[]{:S(2)}, u32[]{:S(2)}) collective-permute-start(bf16[2,4,3,8,2048]{4,3,2,1,0:T(8,128)(2,1)S(1)} %get-tuple-element.29), channel_id=1, source_target_pairs={{0,16},{16,0},{1,17},{17,1},{2,18},{18,2},{3,19},{19,3},{4,20},{20... | collective-permute-start | bytes 2359304 | tf_op jit(solution)/shard_map/ppermute | solution.py:329
  51.9 2.3 %collective-permute-done.other_ref = bf16[2,4,3,8,2048]{4,3,2,1,0:T(8,128)(2,1)S(1)} collective-permute-done((bf16[2,4,3,8,2048]{4,3,2,1,0:T(8,128)(2,1)S(1)}, bf16[2,4,3,8,2048]{4,3,2,1,0:T(8,128)(2,1)S(1)}, u32[]{:S(2)}, u32[]{:S(2)}) %collective-permute-start) | collective-permute-done | bytes 786464 | tf_op jit(solution)/shard_map/ppermute | solution.py:329
  54.1 5.6 %shard_map.103 = (bf16[128,5120]{1,0:T(8,128)(2,1)}, f32[4,3,8,2048]{3,2,1,0:T(8,128)}) custom-call(s32[3]{0:T(128)S(1)} %pad_add_fusion.place_ref, bf16[160,2048]{1,0:T(8,128)(2,1)S(1)} %get-tuple-element.25.grad_ref, bf16[160,384]{1,0:T(8,128)(2,1)S(1)} %get-tuple-element.26.hidden_ref, f32[160,384]{1,0:T(8,128)S(1)} %get-tuple-element.27.gate_ref, ...), custom_call_target="tpu_custom_call" | custom-call | flops 1258291200 | bytes 1048576 | tf_op jit(solution)/shard_map/pallas_call | solution.py:235
  59.8 6.8 %all-to-all-start.1 = ((bf16[16,8,5120]{2,1,0:T(8,128)(2,1)}), bf16[16,8,5120]{2,1,0:T(8,128)(2,1)S(1)}, u32[]{:S(2)}, u32[]{:S(2)}) async-start(bf16[16,8,5120]{2,1,0:T(8,128)(2,1)} %bitcast.23), calls=%async_computation.1 | async-start | bytes 2621440 | tf_op jit(solution)/shard_map/all_to_all | solution.py:283
  66.6 0.0 copy-done.3
  66.6 1.1 shard_map.105
  67.7 0.0 copy-start.4
  67.7 0.0 copy-start.6
  67.7 0.0 copy-start.7
  67.7 3.0 %collective-permute-start.1 = (bf16[4,3,8,2048]{3,2,1,0:T(8,128)(2,1)S(1)}, bf16[4,3,8,2048]{3,2,1,0:T(8,128)(2,1)S(1)}, u32[]{:S(2)}, u32[]{:S(2)}) collective-permute-start(bf16[4,3,8,2048]{3,2,1,0:T(8,128)(2,1)S(1)} %shard_map.105), channel_id=1, source_target_pairs={{0,32},{32,0},{64,96},{96,64},{128,160},{160,128},{192,224},{224,1... | collective-permute-start | bytes 1179656 | tf_op jit(solution)/shard_map/ppermute | solution.py:351
  70.7 9.3 %collective-permute-done.1.came_ref = bf16[4,3,8,2048]{3,2,1,0:T(8,128)(2,1)S(1)} collective-permute-done((bf16[4,3,8,2048]{3,2,1,0:T(8,128)(2,1)S(1)}, bf16[4,3,8,2048]{3,2,1,0:T(8,128)(2,1)S(1)}, u32[]{:S(2)}, u32[]{:S(2)}) %collective-permute-start.1) | collective-permute-done | bytes 393248 | tf_op jit(solution)/shard_map/ppermute | solution.py:351
  80.0 0.1 shard_map.106
  80.1 3.9 %collective-permute-start.2 = (bf16[3,8,2048]{2,1,0:T(8,128)(2,1)S(1)}, bf16[3,8,2048]{2,1,0:T(8,128)(2,1)S(1)}, u32[]{:S(2)}, u32[]{:S(2)}) collective-permute-start(bf16[3,8,2048]{2,1,0:T(8,128)(2,1)S(1)} %get-tuple-element.36), channel_id=1, source_target_pairs={{0,64},{32,96},{64,128},{96,160},{128,192},{160,224},{192,0},{224,... | collective-permute-start | bytes 294920 | tf_op jit(solution)/shard_map/ppermute | solution.py:358
  84.0 5.7 %collective-permute-start.3 = (bf16[3,8,2048]{2,1,0:T(8,128)(2,1)S(1)}, bf16[3,8,2048]{2,1,0:T(8,128)(2,1)S(1)}, u32[]{:S(2)}, u32[]{:S(2)}) collective-permute-start(bf16[3,8,2048]{2,1,0:T(8,128)(2,1)S(1)} %get-tuple-element.37), channel_id=1, source_target_pairs={{0,128},{32,160},{64,192},{96,224},{128,0},{160,32},{192,64},{224,... | collective-permute-start | bytes 294920 | tf_op jit(solution)/shard_map/ppermute | solution.py:358
  89.7 5.0 %collective-permute-start.4 = (bf16[3,8,2048]{2,1,0:T(8,128)(2,1)S(1)}, bf16[3,8,2048]{2,1,0:T(8,128)(2,1)S(1)}, u32[]{:S(2)}, u32[]{:S(2)}) collective-permute-start(bf16[3,8,2048]{2,1,0:T(8,128)(2,1)S(1)} %get-tuple-element.38), channel_id=1, source_target_pairs={{0,192},{32,224},{64,0},{96,32},{128,64},{160,96},{192,128},{224,1... | collective-permute-start | bytes 294920 | tf_op jit(solution)/shard_map/ppermute | solution.py:358
  94.6 0.0 collective-permute-done.2.refs_1_
  94.7 1.5 %collective-permute-done.3.refs_2_ = bf16[3,8,2048]{2,1,0:T(8,128)(2,1)S(1)} collective-permute-done((bf16[3,8,2048]{2,1,0:T(8,128)(2,1)S(1)}, bf16[3,8,2048]{2,1,0:T(8,128)(2,1)S(1)}, u32[]{:S(2)}, u32[]{:S(2)}) %collective-permute-start.3) | collective-permute-done | bytes 98336 | tf_op jit(solution)/shard_map/ppermute | solution.py:358
  96.1 4.6 %collective-permute-done.4.refs_3_ = bf16[3,8,2048]{2,1,0:T(8,128)(2,1)S(1)} collective-permute-done((bf16[3,8,2048]{2,1,0:T(8,128)(2,1)S(1)}, bf16[3,8,2048]{2,1,0:T(8,128)(2,1)S(1)}, u32[]{:S(2)}, u32[]{:S(2)}) %collective-permute-start.4) | collective-permute-done | bytes 98336 | tf_op jit(solution)/shard_map/ppermute | solution.py:358
  100.8 3.4 %collective-permute-start.5 = (bf16[8,2048]{1,0:T(8,128)(2,1)S(1)}, bf16[8,2048]{1,0:T(8,128)(2,1)S(1)}, u32[]{:S(2)}, u32[]{:S(2)}) collective-permute-start(bf16[8,2048]{1,0:T(8,128)(2,1)S(1)} %get-tuple-element.40), channel_id=1, source_target_pairs={{0,256},{256,512},{512,0},{1,257},{257,513},{513,1},{2,258},{258,5... | collective-permute-start | bytes 98312 | tf_op jit(solution)/shard_map/ppermute | solution.py:367
  104.2 5.8 %collective-permute-start.6 = (bf16[8,2048]{1,0:T(8,128)(2,1)S(1)}, bf16[8,2048]{1,0:T(8,128)(2,1)S(1)}, u32[]{:S(2)}, u32[]{:S(2)}) collective-permute-start(bf16[8,2048]{1,0:T(8,128)(2,1)S(1)} %get-tuple-element.41), channel_id=1, source_target_pairs={{0,512},{256,0},{512,256},{1,513},{257,1},{513,257},{2,514},{258,2... | collective-permute-start | bytes 98312 | tf_op jit(solution)/shard_map/ppermute | solution.py:367
  110.0 0.0 collective-permute-done.5
  110.0 2.7 %collective-permute-done.6 = bf16[8,2048]{1,0:T(8,128)(2,1)S(1)} collective-permute-done((bf16[8,2048]{1,0:T(8,128)(2,1)S(1)}, bf16[8,2048]{1,0:T(8,128)(2,1)S(1)}, u32[]{:S(2)}, u32[]{:S(2)}) %collective-permute-start.6) | collective-permute-done | bytes 32800 | tf_op jit(solution)/shard_map/ppermute | solution.py:367
  112.8 0.6 fusion
  113.4 0.0 all-to-all-done.1
  113.4 1.6 %shard_map.104 = (bf16[128,2048]{1,0:T(8,128)(2,1)}, bf16[128,2048]{1,0:T(8,128)(2,1)}, f32[1,128]{1,0:T(1,128)}) custom-call(s32[8,128]{1,0:T(8,128)S(1)} %copy-done.6, f32[1,128]{1,0:T(1,128)S(1)} %bitcast.21, bf16[128,2048]{1,0:T(8,128)(2,1)S(1)} %copy-done.4, bf16[128,5120]{1,0:T(8,128)(2,1)S(1)} %bitcast.19), custom_call_target="tpu_custom_call" | custom-call | bytes 1048576 | tf_op jit(solution)/shard_map/pallas_call | solution.py:235
  (11 shorter events, 0.1 us)
Async XLA Ops:
  0.6 45.9 %copy-start.1 = (bf16[1,2048,384]{2,1,0:T(8,128)(2,1)S(1)}, bf16[1,2048,384]{2,1,0:T(8,128)(2,1)}, u32[]{:S(2)}) copy-start(bf16[1,2048,384]{2,1,0:T(8,128)(2,1)} %param.11) | copy-start | bytes 4718596
  4.9 41.7 %copy-start = (bf16[1,2048,384]{2,1,0:T(8,128)(2,1)S(1)}, bf16[1,2048,384]{2,1,0:T(8,128)(2,1)}, u32[]{:S(2)}) copy-start(bf16[1,2048,384]{2,1,0:T(8,128)(2,1)} %param.10) | copy-start | bytes 4718596
  4.9 41.7 %all-to-all-start = ((bf16[16,8,5120]{2,1,0:T(8,128)(2,1)}), bf16[16,8,5120]{2,1,0:T(8,128)(2,1)}, u32[]{:S(2)}, u32[]{:S(2)}) async-start(bf16[16,8,5120]{2,1,0:T(8,128)(2,1)} %bitcast.24), calls=%async_computation | async-start | bytes 2621440 | tf_op jit(solution)/shard_map/all_to_all | solution.py:283
  49.9 9.8 %copy-start.2 = (bf16[160,2048]{1,0:T(8,128)(2,1)}, bf16[160,2048]{1,0:T(8,128)(2,1)S(1)}, u32[]{:S(2)}) copy-start(bf16[160,2048]{1,0:T(8,128)(2,1)S(1)} %get-tuple-element.25.grad_ref) | copy-start | bytes 1966084
  49.9 4.2 %collective-permute-start = (bf16[2,4,3,8,2048]{4,3,2,1,0:T(8,128)(2,1)S(1)}, bf16[2,4,3,8,2048]{4,3,2,1,0:T(8,128)(2,1)S(1)}, u32[]{:S(2)}, u32[]{:S(2)}) collective-permute-start(bf16[2,4,3,8,2048]{4,3,2,1,0:T(8,128)(2,1)S(1)} %get-tuple-element.29), channel_id=1, source_target_pairs={{0,16},{16,0},{1,17},{17,1},{2,18},{18,2},{3,19},{19,3},{4,20},{20... | collective-permute-start | bytes 2359304 | tf_op jit(solution)/shard_map/ppermute | solution.py:329
  59.8 6.8 %copy-start.3 = (bf16[160,2048]{1,0:T(8,128)(2,1)S(1)}, bf16[160,2048]{1,0:T(8,128)(2,1)}, u32[]{:S(2)}) copy-start(bf16[160,2048]{1,0:T(8,128)(2,1)} %copy-done.2) | copy-start | bytes 1966084
  59.8 53.6 %all-to-all-start.1 = ((bf16[16,8,5120]{2,1,0:T(8,128)(2,1)}), bf16[16,8,5120]{2,1,0:T(8,128)(2,1)S(1)}, u32[]{:S(2)}, u32[]{:S(2)}) async-start(bf16[16,8,5120]{2,1,0:T(8,128)(2,1)} %bitcast.23), calls=%async_computation.1 | async-start | bytes 2621440 | tf_op jit(solution)/shard_map/all_to_all | solution.py:283
  66.6 13.4 %copy-start.5 = (f32[4,3,8,2048]{3,2,1,0:T(8,128)S(1)}, f32[4,3,8,2048]{3,2,1,0:T(8,128)}, u32[]{:S(2)}) copy-start(f32[4,3,8,2048]{3,2,1,0:T(8,128)} %get-tuple-element.34.own_ref) | copy-start | bytes 2359300
  67.7 45.7 %copy-start.4 = (bf16[128,2048]{1,0:T(8,128)(2,1)S(1)}, bf16[128,2048]{1,0:T(8,128)(2,1)}, u32[]{:S(2)}) copy-start(bf16[128,2048]{1,0:T(8,128)(2,1)} %cot_ref.3) | copy-start | bytes 1572868
  67.7 45.7 %copy-start.6 = (s32[8,128]{1,0:T(8,128)S(1)}, s32[8,128]{1,0:T(8,128)}, u32[]{:S(2)}) copy-start(s32[8,128]{1,0:T(8,128)} %get-tuple-element.23.rows_ref) | copy-start | bytes 12292
  67.7 45.7 %copy-start.7 = (f32[128,1]{0,1:T(1,128)S(1)}, f32[128,1]{0,1:T(1,128)}, u32[]{:S(2)}) copy-start(f32[128,1]{0,1:T(1,128)} %param.9) | copy-start | bytes 1540
  67.7 12.3 %collective-permute-start.1 = (bf16[4,3,8,2048]{3,2,1,0:T(8,128)(2,1)S(1)}, bf16[4,3,8,2048]{3,2,1,0:T(8,128)(2,1)S(1)}, u32[]{:S(2)}, u32[]{:S(2)}) collective-permute-start(bf16[4,3,8,2048]{3,2,1,0:T(8,128)(2,1)S(1)} %shard_map.105), channel_id=1, source_target_pairs={{0,32},{32,0},{64,96},{96,64},{128,160},{160,128},{192,224},{224,1... | collective-permute-start | bytes 1179656 | tf_op jit(solution)/shard_map/ppermute | solution.py:351
  80.1 14.6 %collective-permute-start.2 = (bf16[3,8,2048]{2,1,0:T(8,128)(2,1)S(1)}, bf16[3,8,2048]{2,1,0:T(8,128)(2,1)S(1)}, u32[]{:S(2)}, u32[]{:S(2)}) collective-permute-start(bf16[3,8,2048]{2,1,0:T(8,128)(2,1)S(1)} %get-tuple-element.36), channel_id=1, source_target_pairs={{0,64},{32,96},{64,128},{96,160},{128,192},{160,224},{192,0},{224,... | collective-permute-start | bytes 294920 | tf_op jit(solution)/shard_map/ppermute | solution.py:358
  84.0 12.1 %collective-permute-start.3 = (bf16[3,8,2048]{2,1,0:T(8,128)(2,1)S(1)}, bf16[3,8,2048]{2,1,0:T(8,128)(2,1)S(1)}, u32[]{:S(2)}, u32[]{:S(2)}) collective-permute-start(bf16[3,8,2048]{2,1,0:T(8,128)(2,1)S(1)} %get-tuple-element.37), channel_id=1, source_target_pairs={{0,128},{32,160},{64,192},{96,224},{128,0},{160,32},{192,64},{224,... | collective-permute-start | bytes 294920 | tf_op jit(solution)/shard_map/ppermute | solution.py:358
  89.7 11.1 %collective-permute-start.4 = (bf16[3,8,2048]{2,1,0:T(8,128)(2,1)S(1)}, bf16[3,8,2048]{2,1,0:T(8,128)(2,1)S(1)}, u32[]{:S(2)}, u32[]{:S(2)}) collective-permute-start(bf16[3,8,2048]{2,1,0:T(8,128)(2,1)S(1)} %get-tuple-element.38), channel_id=1, source_target_pairs={{0,192},{32,224},{64,0},{96,32},{128,64},{160,96},{192,128},{224,1... | collective-permute-start | bytes 294920 | tf_op jit(solution)/shard_map/ppermute | solution.py:358
  100.8 9.2 %collective-permute-start.5 = (bf16[8,2048]{1,0:T(8,128)(2,1)S(1)}, bf16[8,2048]{1,0:T(8,128)(2,1)S(1)}, u32[]{:S(2)}, u32[]{:S(2)}) collective-permute-start(bf16[8,2048]{1,0:T(8,128)(2,1)S(1)} %get-tuple-element.40), channel_id=1, source_target_pairs={{0,256},{256,512},{512,0},{1,257},{257,513},{513,1},{2,258},{258,5... | collective-permute-start | bytes 98312 | tf_op jit(solution)/shard_map/ppermute | solution.py:367
  104.2 8.6 %collective-permute-start.6 = (bf16[8,2048]{1,0:T(8,128)(2,1)S(1)}, bf16[8,2048]{1,0:T(8,128)(2,1)S(1)}, u32[]{:S(2)}, u32[]{:S(2)}) collective-permute-start(bf16[8,2048]{1,0:T(8,128)(2,1)S(1)} %get-tuple-element.41), channel_id=1, source_target_pairs={{0,512},{256,0},{512,256},{1,513},{257,1},{513,257},{2,514},{258,2... | collective-permute-start | bytes 98312 | tf_op jit(solution)/shard_map/ppermute | solution.py:367
